TPU v7x, 32 devices: a whole 2x2x4 slice. The times are simulated.
32 devices in a mesh: dp: 8 (over z, x), tensor: 4 (over y, core).
Axes of the slice: x: 2, y: 2, z: 4, core: 2. Of those that a mesh axis runs over, the one named last changes fastest.
Arguments:
- stream_in: bfloat16 [8, 1024, 2048], P('dp', 'tensor'), may hold values from -6 to 6
- segments: int32 [8, 1024], P('dp'), may hold values from 0 to 2, never falling along the last dimension, each value on 1 to 800 neighbouring positions
- first_gain: float32 [2048], replicated, may hold values from 0.5 to 1.5
- gelu_gate_weight: bfloat16 [2048, 2560], P(None, 'tensor'), may hold values from -0.125 to 0.125
- recurrent_branch_weight: bfloat16 [2048, 2560], P(None, 'tensor'), may hold values from -0.125 to 0.125
- conv_kernel: float32 [4, 2560], P(None, 'tensor'), may hold values from -3 to 3
- conv_bias: float32 [2560], P('tensor'), may hold values from -3 to 3
- recur_weight: bfloat16 [16, 160, 160], P('tensor'), may hold values from -0.5 to 0.5
- recur_bias: float32 [2560], P('tensor'), may hold values from -4 to 4
- inlet_weight: bfloat16 [16, 160, 160], P('tensor'), may hold values from -0.5 to 0.5
- inlet_bias: float32 [2560], P('tensor'), may hold values from -3 to 3
- decay_param: float32 [2560], P('tensor'), may hold values from 5 to 9
- recurrent_output_weight: bfloat16 [2560, 2048], P('tensor'), may hold values from -0.25 to 0.25
- second_gain: float32 [2048], replicated, may hold values from 0.5 to 1.5
- gate_projection_weight: bfloat16 [2048, 6144], P(None, 'tensor'), may hold values from -0.125 to 0.125
- up_projection_weight: bfloat16 [2048, 6144], P(None, 'tensor'), may hold values from -0.125 to 0.125
- down_projection_weight: bfloat16 [6144, 2048], P('tensor'), may hold values from -0.15625 to 0.15625
- cotangent: bfloat16 [8, 1024, 2048], P('dp', 'tensor'), may hold values from -6 to 6
Outputs:
- stream_out: float32 [8, 1024, 2048], P('dp', 'tensor')
- stream_grad: float32 [8, 1024, 2048], P('dp', 'tensor')
- first_gain_grad: float32 [2048], replicated
- gated_weight_grad: float32 [2048, 2560], P('dp', 'tensor')
- branch_weight_grad: float32 [2048, 2560], P('dp', 'tensor')
- conv_kernel_grad: float32 [4, 2560], P(None, 'tensor')
- conv_bias_grad: float32 [2560], P('tensor')
- recur_weight_grad: float32 [16, 160, 160], P('tensor')
- recur_bias_grad: float32 [2560], P('tensor')
- inlet_weight_grad: float32 [16, 160, 160], P('tensor')
- inlet_bias_grad: float32 [2560], P('tensor')
- decay_param_grad: float32 [2560], P('tensor')
- output_weight_grad: float32 [2560, 2048], P('tensor', 'dp')
- second_gain_grad: float32 [2048], replicated
- hidden_gate_grad: float32 [2048, 6144], P('dp', 'tensor')
- hidden_up_grad: float32 [2048, 6144], P('dp', 'tensor')
- hidden_down_grad: float32 [6144, 2048], P('tensor', 'dp')
Inputs may be any that keep to these rules, and one draw needn't show every extreme that they name: `segments`: segment numbers never fall along a sequence; a document starts at position 0 and wherever the number changes, and no document is longer than 800 tokens.
All inputs are finite; a program needn't handle non-finite values.
Results may differ from a plain program's by a relative error of at most 0.0085.
Values may be sent and summed in bfloat16 or wider, within the bound.
A program may use at most 256 MiB of HBM per device.

v0:
```python
import jax
import jax.numpy as jnp
from jax import lax
from jax.sharding import PartitionSpec as P

epsilon = 1e-06
decay_scale = 8.0


def rms_apply(values, gain_vec):
    inverse_rms = lax.rsqrt(jnp.mean(values * values, axis=-1, keepdims=True) + epsilon)
    return values * inverse_rms * gain_vec


def gelu_tanh(values):
    return jax.nn.gelu(values, approximate=True)


def segment_masks(segments, taps):
    seq_len = segments.shape[1]
    padded = jnp.pad(segments, ((0, 0), (taps - 1, 0)), constant_values=-1)
    same_list = []
    for offset in range(1, taps):
        earlier = padded[:, taps - 1 - offset : taps - 1 - offset + seq_len]
        same_list.append((earlier == segments).astype(jnp.float32)[..., None])
    starts = 1.0 - same_list[0]
    return (starts, same_list)


def causal_conv(inputs, kernel, bias_vec, same_list):
    summed = bias_vec + kernel[0] * inputs
    for offset in range(1, kernel.shape[0]):
        shifted = jnp.pad(inputs, ((0, 0), (offset, 0), (0, 0)))[:, :-offset]
        summed = summed + kernel[offset] * shifted * same_list[offset - 1]
    return summed


def combine_pairs(earlier, latter):
    return (earlier[0] * latter[0], latter[0] * earlier[1] + latter[1])


def recurrence(recur_pre, inlet_pre, inputs, decay_param, starts):
    forget_rate = jax.nn.sigmoid(recur_pre)
    log_a = -decay_scale * forget_rate * jax.nn.softplus(-decay_param)
    decay_step = jnp.exp(log_a)
    norm_factor = jnp.sqrt(-jnp.expm1(2.0 * log_a))
    multiplier = starts + (1.0 - starts) * norm_factor
    carried = decay_step * (1.0 - starts)
    driven = multiplier * jax.nn.sigmoid(inlet_pre) * inputs
    _, states = lax.associative_scan(combine_pairs, (carried, driven), axis=1)
    return states


def on_device(
    stream_in,
    segments,
    first_gain,
    gelu_gate_weight,
    recurrent_branch_weight,
    conv_kernel,
    conv_bias,
    recur_weight,
    recur_bias,
    inlet_weight,
    inlet_bias,
    decay_param,
    recurrent_output_weight,
    second_gain,
    gate_projection_weight,
    up_projection_weight,
    down_projection_weight,
    cotangent,
):
    values = stream_in.astype(jnp.float32)
    seq_count, part_len, model_width = values.shape
    full_len = segments.shape[1]
    head_count, block_width = (recur_weight.shape[0], recur_weight.shape[1])
    starts, same_list = segment_masks(segments, conv_kernel.shape[0])
    normed_f, first_back = jax.vjp(rms_apply, values, first_gain)
    normalized_input = lax.all_gather(normed_f.astype(jnp.bfloat16), "tensor", axis=1, tiled=True)
    gated_preactivation = jnp.einsum(
        "hqg,gz->hqz", normalized_input, gelu_gate_weight, preferred_element_type=jnp.float32
    )
    branch_pre = jnp.einsum(
        "hqg,gz->hqz", normalized_input, recurrent_branch_weight, preferred_element_type=jnp.float32
    )
    conv_f, conv_back = jax.vjp(
        lambda b, k, c: causal_conv(b, k, c, same_list), branch_pre, conv_kernel, conv_bias
    )
    conv_out = conv_f.astype(jnp.bfloat16)
    head_split = conv_out.reshape(seq_count, full_len, head_count, block_width)
    recur_pre = (
        jnp.einsum(
            "slhi,hij->slhj", head_split, recur_weight, preferred_element_type=jnp.float32
        ).reshape(seq_count, full_len, -1)
        + recur_bias
    )
    inlet_pre = (
        jnp.einsum(
            "slhi,hij->slhj", head_split, inlet_weight, preferred_element_type=jnp.float32
        ).reshape(seq_count, full_len, -1)
        + inlet_bias
    )
    states, recur_back = jax.vjp(
        lambda a, i, u, d: recurrence(a, i, u, d, starts),
        recur_pre,
        inlet_pre,
        conv_out.astype(jnp.float32),
        decay_param,
    )
    activated, gelu_back = jax.vjp(gelu_tanh, gated_preactivation)
    gated_product = (states * activated).astype(jnp.bfloat16)
    row_block = gated_product
    attended = lax.psum_scatter(
        jnp.einsum(
            "slr,rd->lsd", row_block, recurrent_output_weight, preferred_element_type=jnp.float32
        ),
        "tensor",
        scatter_dimension=0,
        tiled=True,
    )
    middle = values + jnp.transpose(attended, (1, 0, 2))
    normed_two_f, second_back = jax.vjp(rms_apply, middle, second_gain)
    normalized_second = lax.all_gather(
        normed_two_f.astype(jnp.bfloat16), "tensor", axis=1, tiled=True
    )
    gate_pre = jnp.einsum(
        "vti,ig->vtg", normalized_second, gate_projection_weight, preferred_element_type=jnp.float32
    )
    up_preactivation = jnp.einsum(
        "vti,ig->vtg", normalized_second, up_projection_weight, preferred_element_type=jnp.float32
    )
    gate_act, ffn_gelu_back = jax.vjp(gelu_tanh, gate_pre)
    hidden_activation = (gate_act * up_preactivation).astype(jnp.bfloat16)
    row_block = hidden_activation
    ffn_out = lax.psum_scatter(
        jnp.einsum(
            "slf,fd->lsd", row_block, down_projection_weight, preferred_element_type=jnp.float32
        ).astype(jnp.bfloat16),
        "tensor",
        scatter_dimension=0,
        tiled=True,
    ).astype(jnp.float32)
    stream_out = middle + jnp.transpose(ffn_out, (1, 0, 2))
    cotangent_whole = lax.all_gather(cotangent, "tensor", axis=1, tiled=True)
    down_weight_gradient = jnp.einsum(
        "nym,nye->me", hidden_activation, cotangent_whole, preferred_element_type=jnp.float32
    )
    hidden_gradient = jnp.einsum(
        "yqr,mr->yqm", cotangent_whole, down_projection_weight, preferred_element_type=jnp.float32
    )
    gate_gradient = ffn_gelu_back(hidden_gradient * up_preactivation)[0].astype(jnp.bfloat16)
    up_gradient = (hidden_gradient * gate_act).astype(jnp.bfloat16)
    gate_weight_gradient = jnp.einsum(
        "vzo,vze->oe", normalized_second, gate_gradient, preferred_element_type=jnp.float32
    )
    up_weight_gradient = jnp.einsum(
        "vzo,vze->oe", normalized_second, up_gradient, preferred_element_type=jnp.float32
    )
    d_normed_two = jnp.transpose(
        lax.psum_scatter(
            jnp.einsum(
                "slf,df->lsd",
                gate_gradient,
                gate_projection_weight,
                preferred_element_type=jnp.float32,
            )
            + jnp.einsum(
                "slf,df->lsd", up_gradient, up_projection_weight, preferred_element_type=jnp.float32
            ),
            "tensor",
            scatter_dimension=0,
            tiled=True,
        ),
        (1, 0, 2),
    )
    d_middle_norm, grad_second = second_back(d_normed_two)
    d_middle = cotangent.astype(jnp.float32) + d_middle_norm
    attended_gradient = lax.all_gather(d_middle.astype(jnp.bfloat16), "tensor", axis=1, tiled=True)
    output_weight_gradient = jnp.einsum(
        "fbe,fbk->ek", gated_product, attended_gradient, preferred_element_type=jnp.float32
    )
    d_product = jnp.einsum(
        "mkz,jz->mkj",
        attended_gradient,
        recurrent_output_weight,
        preferred_element_type=jnp.float32,
    )
    d_states = d_product * activated
    d_activated = d_product * states
    d_recur, d_inlet, d_conv_rec, grad_decay = recur_back(d_states)
    d_recur_low = d_recur.astype(jnp.bfloat16)
    d_inlet_low = d_inlet.astype(jnp.bfloat16)
    grad_recur_bias = jnp.sum(d_recur_low.astype(jnp.float32), axis=(0, 1))
    grad_inlet_bias = jnp.sum(d_inlet_low.astype(jnp.float32), axis=(0, 1))
    recur_heads = d_recur_low.reshape(seq_count, full_len, head_count, block_width)
    inlet_heads = d_inlet_low.reshape(seq_count, full_len, head_count, block_width)
    grad_recur = jnp.einsum(
        "slhi,slhj->hij", head_split, recur_heads, preferred_element_type=jnp.float32
    )
    grad_inlet = jnp.einsum(
        "slhi,slhj->hij", head_split, inlet_heads, preferred_element_type=jnp.float32
    )
    gate_back = jnp.einsum(
        "slhj,hij->slhi", recur_heads, recur_weight, preferred_element_type=jnp.float32
    ) + jnp.einsum("slhj,hij->slhi", inlet_heads, inlet_weight, preferred_element_type=jnp.float32)
    d_conv = d_conv_rec + gate_back.reshape(seq_count, full_len, -1)
    d_branch, grad_kernel, grad_conv_bias = conv_back(d_conv)
    gated_gradient = gelu_back(d_activated)[0].astype(jnp.bfloat16)
    branch_gradient_lowered = d_branch.astype(jnp.bfloat16)
    gated_weight_gradient = jnp.einsum(
        "uft,ufe->te", normalized_input, gated_gradient, preferred_element_type=jnp.float32
    )
    grad_branch = jnp.einsum(
        "uft,ufe->te", normalized_input, branch_gradient_lowered, preferred_element_type=jnp.float32
    )
    d_normed = jnp.transpose(
        lax.psum_scatter(
            jnp.einsum(
                "slr,dr->lsd", gated_gradient, gelu_gate_weight, preferred_element_type=jnp.float32
            )
            + jnp.einsum(
                "slr,dr->lsd",
                branch_gradient_lowered,
                recurrent_branch_weight,
                preferred_element_type=jnp.float32,
            ),
            "tensor",
            scatter_dimension=0,
            tiled=True,
        ),
        (1, 0, 2),
    )
    d_values_norm, grad_first = first_back(d_normed)
    stream_grad = d_middle + d_values_norm
    grad_first, grad_second = lax.psum((grad_first, grad_second), ("dp", "tensor"))
    (
        grad_kernel,
        grad_conv_bias,
        grad_recur,
        grad_recur_bias,
        grad_inlet,
        grad_inlet_bias,
        grad_decay,
    ) = lax.psum(
        (
            grad_kernel,
            grad_conv_bias,
            grad_recur,
            grad_recur_bias,
            grad_inlet,
            grad_inlet_bias,
            grad_decay,
        ),
        "dp",
    )
    (
        gated_weight_gradient,
        grad_branch,
        output_weight_gradient,
        gate_weight_gradient,
        up_weight_gradient,
        down_weight_gradient,
    ) = (
        lax.psum_scatter(gated_weight_gradient, "dp", scatter_dimension=0, tiled=True),
        lax.psum_scatter(grad_branch, "dp", scatter_dimension=0, tiled=True),
        lax.psum_scatter(output_weight_gradient, "dp", scatter_dimension=1, tiled=True),
        lax.psum_scatter(gate_weight_gradient, "dp", scatter_dimension=0, tiled=True),
        lax.psum_scatter(up_weight_gradient, "dp", scatter_dimension=0, tiled=True),
        lax.psum_scatter(down_weight_gradient, "dp", scatter_dimension=1, tiled=True),
    )
    return (
        stream_out,
        stream_grad,
        grad_first,
        gated_weight_gradient,
        grad_branch,
        grad_kernel,
        grad_conv_bias,
        grad_recur,
        grad_recur_bias,
        grad_inlet,
        grad_inlet_bias,
        grad_decay,
        output_weight_gradient,
        grad_second,
        gate_weight_gradient,
        up_weight_gradient,
        down_weight_gradient,
    )


def solution(mesh):
    in_specs = (
        P("dp", "tensor", None),
        P("dp", None),
        P(),
        P(None, "tensor"),
        P(None, "tensor"),
        P(None, "tensor"),
        P("tensor"),
        P("tensor", None, None),
        P("tensor"),
        P("tensor", None, None),
        P("tensor"),
        P("tensor"),
        P("tensor", None),
        P(),
        P(None, "tensor"),
        P(None, "tensor"),
        P("tensor", None),
        P("dp", "tensor", None),
    )
    out_specs = (
        P("dp", "tensor", None),
        P("dp", "tensor", None),
        P(),
        P("dp", "tensor"),
        P("dp", "tensor"),
        P(None, "tensor"),
        P("tensor"),
        P("tensor", None, None),
        P("tensor"),
        P("tensor", None, None),
        P("tensor"),
        P("tensor"),
        P("tensor", "dp"),
        P(),
        P("dp", "tensor"),
        P("dp", "tensor"),
        P("tensor", "dp"),
    )
    return jax.shard_map(
        on_device, mesh=mesh, in_specs=in_specs, out_specs=out_specs, check_vma=False
    )
```

profile of v0, /device:TPU:0, one launch (start us, length us, event | category | flops | bytes accessed | tf_op | source)
XLA Modules:
  0.0 1981.5 jit_solution(5432334179395999616)
XLA Ops:
  12.5 37.0 %all-gather.5.cloned.1.call-done = bf16[1,1024,2048]{2,1,0:T(8,128)(2,1)} async-done(((bf16[1,256,2048]{2,1,0:T(8,128)(2,1)}), bf16[1,1024,2048]{2,1,0:T(8,128)(2,1)}) %all-gather.5.cloned.1.call-update) | async-done | bytes 4194320 | tf_op jit(solution)/shard_map/all_gather | solution.py:80
  272.5 9.1 pad.445
  285.6 9.1 pad.444
  310.1 71.8 %reduce-scatter.11.cloned.1.call-done = f32[256,1,2048]{2,0,1:T(8,128)} async-done(((f32[1024,1,2048]{2,0,1:T(8,128)}), f32[256,1,2048]{2,0,1:T(8,128)}) %reduce-scatter.11.cloned.1.call-update) | async-done | bytes 2097168 | tf_op jit(solution)/shard_map/reduce_scatter | solution.py:114
  387.4 34.0 %all-gather.7.cloned.1.call-done = bf16[1,1024,2048]{2,1,0:T(8,128)(2,1)} async-done(((bf16[1,256,2048]{2,1,0:T(8,128)(2,1)}), bf16[1,1024,2048]{2,1,0:T(8,128)(2,1)}) %all-gather.7.cloned.1.call-update) | async-done | bytes 4194320 | tf_op jit(solution)/shard_map/all_gather | solution.py:124
  421.4 12.5 fusion.19
  433.9 10.5 fusion.21
  444.3 13.0 all-gather.9.cloned.1.call-done
  457.4 18.0 multiply_convert_fusion
  475.4 11.1 fusion.142
  486.5 11.1 add_bitcast_fusion.1
  497.6 71.8 %reduce-scatter.15.cloned.1.call-done = f32[256,1,2048]{2,0,1:T(8,128)} async-done(((f32[1024,1,2048]{2,0,1:T(8,128)}), f32[256,1,2048]{2,0,1:T(8,128)}) %reduce-scatter.15.cloned.1.call-update) | async-done | bytes 2097168 | tf_op jit(solution)/shard_map/reduce_scatter | solution.py:161
  577.3 34.6 %all-gather.11.cloned.1.call-done = bf16[1,1024,2048]{2,1,0:T(8,128)(2,1)} async-done(((bf16[1,256,2048]{2,1,0:T(8,128)(2,1)}), bf16[1,1024,2048]{2,1,0:T(8,128)(2,1)}) %all-gather.11.cloned.1.call-update) | async-done | bytes 4194320 | tf_op jit(solution)/shard_map/all_gather | solution.py:179
  611.9 9.6 fusion.42
  722.7 9.3 pad.539
  748.1 9.4 pad.513
  757.6 9.4 multiply_reduce_fusion
  784.9 9.9 multiply_reduce_fusion.4
  808.5 11.1 convert_bitcast_fusion
  825.1 12.5 fusion.17
  837.7 12.5 fusion.15
  850.2 12.7 fusion.11
  882.4 8.1 fusion.25
  890.7 38.0 %all-reduce.107 = (f32[4,640]{1,0:T(4,128)}, f32[640]{0:T(1024)}, f32[640]{0:T(1024)}, f32[640]{0:T(1024)}, f32[640]{0:T(1024)}) all-reduce(f32[4,640]{1,0:T(4,128)S(1)} %pad_add_fusion.8, f32[640]{0:T(1024)S(1)} %get-tuple-element.24, f32[640]{0:T(1024)S(1)} %get-tuple-element.76, ...), channel_id=1, replica_groups=mesh['dp'=8,'tensor'=4] {'dp'}, use_global_device_ids=true, to_apply=%region_16.17 | all-reduce | flops 5120 | bytes 40960 | tf_op jit(solution)/shard_map/psum | solution.py:245
  931.0 38.6 %all-reduce.106 = (f32[2048]{0:T(1024)}, f32[2048]{0:T(1024)}) all-reduce(f32[2048]{0:T(1024)S(1)} %get-tuple-element.22, f32[2048]{0:T(1024)S(1)} %copy-done.138), channel_id=1, replica_groups=mesh['dp'=8,'tensor'=4] {'dp','tensor'}, use_global_device_ids=true, to_apply=%region_9.10 | all-reduce | flops 4096 | bytes 32768 | tf_op jit(solution)/shard_map/psum | solution.py:236
  976.7 40.3 %all-reduce.111.cloned.1.call-done = (f32[4,160,160]{2,1,0:T(8,128)}, f32[4,160,160]{2,1,0:T(8,128)}) async-done(((f32[4,160,160]{2,1,0:T(8,128)}, f32[4,160,160]{2,1,0:T(8,128)}), (f32[4,160,160]{2,1,0:T(8,128)}, f32[4,160,160]{2,1,0:T(8,128)})) %all-reduce.111.cloned.1.call-update) | async-done | bytes 819216 | tf_op jit(solution)/shard_map/psum | solution.py:245
  1016.9 211.0 %reduce-scatter.25.cloned.1.call-done = f32[256,1536]{1,0:T(8,128)} async-done(((f32[2048,1536]{1,0:T(8,128)}), f32[256,1536]{1,0:T(8,128)}) %reduce-scatter.25.cloned.1.call-update) | async-done | bytes 1572880 | tf_op jit(solution)/shard_map/reduce_scatter | solution.py:268
  1227.9 211.1 %reduce-scatter.27.cloned.1.call-done = f32[256,1536]{1,0:T(8,128)} async-done(((f32[2048,1536]{1,0:T(8,128)}), f32[256,1536]{1,0:T(8,128)}) %reduce-scatter.27.cloned.1.call-update) | async-done | bytes 1572880 | tf_op jit(solution)/shard_map/reduce_scatter | solution.py:269
  1439.0 211.3 %reduce-scatter.29.cloned.1.call-done = f32[1536,256]{1,0:T(8,128)} async-done(((f32[1536,2048]{1,0:T(8,128)}), f32[1536,256]{1,0:T(8,128)}) %reduce-scatter.29.cloned.1.call-update) | async-done | bytes 1572880 | tf_op jit(solution)/shard_map/reduce_scatter | solution.py:270
  1650.3 106.3 %reduce-scatter.21.cloned.1.call-done = f32[256,640]{1,0:T(8,128)} async-done(((f32[2048,640]{1,0:T(8,128)}), f32[256,640]{1,0:T(8,128)}) %reduce-scatter.21.cloned.1.call-update) | async-done | bytes 655376 | tf_op jit(solution)/shard_map/reduce_scatter | solution.py:266
  1756.5 107.2 %reduce-scatter.23.cloned.1.call-done = f32[640,256]{1,0:T(8,128)} async-done(((f32[640,2048]{1,0:T(8,128)}), f32[640,256]{1,0:T(8,128)}) %reduce-scatter.23.cloned.1.call-update) | async-done | bytes 655376 | tf_op jit(solution)/shard_map/reduce_scatter | solution.py:267
  1863.8 106.7 %reduce-scatter.19.cloned.1.call-done = f32[256,640]{1,0:T(8,128)} async-done(((f32[2048,640]{1,0:T(8,128)}), f32[256,640]{1,0:T(8,128)}) %reduce-scatter.19.cloned.1.call-update) | async-done | bytes 655376 | tf_op jit(solution)/shard_map/reduce_scatter | solution.py:265
  (659 shorter events, 446.1 us)
Async XLA Ops:
  7.2 297.3 %copy-start = (bf16[640,2048]{1,0:T(8,128)(2,1)S(1)}, bf16[640,2048]{1,0:T(8,128)(2,1)}, u32[]{:S(2)}) copy-start(bf16[640,2048]{1,0:T(8,128)(2,1)} %param.30) | copy-start | bytes 7864324
  7.2 42.2 %all-gather.5.cloned.1.call-start = ((), (), s32[]{:S(2)}) async-start(), calls=%async_computation.10 | async-start | bytes 5242880 | tf_op jit(solution)/shard_map/all_gather | solution.py:80
  12.1 369.9 %reduce-scatter.11.cloned.1.call-start = ((), (), s32[]{:S(2)}) async-start(), calls=%async_computation.11 | async-start | bytes 10485760 | tf_op jit(solution)/shard_map/reduce_scatter | solution.py:114
  12.2 43.2 %copy-start.130 = (f32[640]{0:T(1024)}, f32[640]{0:T(1024)S(1)}, u32[]{:S(2)}) copy-start(f32[640]{0:T(1024)S(1)} %get-tuple-element.26) | copy-start | bytes 7684
  12.2 43.2 %copy-start.132 = (f32[640]{0:T(1024)}, f32[640]{0:T(1024)S(1)}, u32[]{:S(2)}) copy-start(f32[640]{0:T(1024)S(1)} %get-tuple-element.27) | copy-start | bytes 7684
  12.3 63.1 %copy-start.100 = (f32[640]{0:T(1024)}, f32[640]{0:T(1024)S(1)}, u32[]{:S(2)}) copy-start(f32[640]{0:T(1024)S(1)} %broadcast_multiply_fusion) | copy-start | bytes 7684
  12.4 63.0 %copy-start.102 = (f32[1024]{0:T(1024)}, f32[1024]{0:T(1024)S(1)}, u32[]{:S(2)}) copy-start(f32[1024]{0:T(1024)S(1)} %get-tuple-element.170) | copy-start | bytes 12292
  12.4 63.0 %copy-start.117 = (f32[1024]{0:T(1024)}, f32[1024]{0:T(1024)S(1)}, u32[]{:S(2)}) copy-start(f32[1024]{0:T(1024)S(1)} %get-tuple-element.169) | copy-start | bytes 12292
  12.5 44.5 %copy-start.161 = (f32[640]{0:T(1024)S(1)}, f32[640]{0:T(1024)}, u32[]{:S(2)}) copy-start(f32[640]{0:T(1024)} %param.24) | copy-start | bytes 7684
  148.5 64.3 %copy-start.48 = (f32[1,64,640]{2,1,0:T(8,128)}, f32[1,64,640]{2,1,0:T(8,128)S(1)}, u32[]{:S(2)}) copy-start(f32[1,64,640]{2,1,0:T(8,128)S(1)} %slice.369) | copy-start | bytes 491524
  155.2 57.6 %copy-start.38 = (f32[1,256,640]{2,1,0:T(8,128)S(1)}, f32[1,256,640]{2,1,0:T(8,128)}, u32[]{:S(2)}) copy-start(f32[1,256,640]{2,1,0:T(8,128)} %get-tuple-element.102) | copy-start | bytes 1966084
  156.2 62.9 %copy-start.61 = (f32[1,32,640]{2,1,0:T(8,128)}, f32[1,32,640]{2,1,0:T(8,128)S(1)}, u32[]{:S(2)}) copy-start(f32[1,32,640]{2,1,0:T(8,128)S(1)} %slice.375) | copy-start | bytes 245764
  170.5 52.9 %copy-start.86 = (f32[1,8,640]{2,1,0:T(8,128)}, f32[1,8,640]{2,1,0:T(8,128)S(1)}, u32[]{:S(2)}) copy-start(f32[1,8,640]{2,1,0:T(8,128)S(1)} %slice.387) | copy-start | bytes 61444
  176.7 46.7 %copy-start.95 = (f32[1,4,640]{2,1,0:T(4,128)}, f32[1,4,640]{2,1,0:T(4,128)S(1)}, u32[]{:S(2)}) copy-start(f32[1,4,640]{2,1,0:T(4,128)S(1)} %slice.393) | copy-start | bytes 30724
  310.1 111.3 %all-gather.7.cloned.1.call-start = ((), (), s32[]{:S(2)}) async-start(), calls=%async_computation.12 | async-start | bytes 5242880 | tf_op jit(solution)/shard_map/all_gather | solution.py:124
  386.7 70.6 %all-gather.9.cloned.1.call-start = ((), (), s32[]{:S(2)}) async-start(), calls=%async_computation.14 | async-start | bytes 5242880 | tf_op jit(solution)/shard_map/all_gather | solution.py:145
  387.3 182.1 %reduce-scatter.15.cloned.1.call-start = ((), (), s32[]{:S(2)}) async-start(), calls=%async_computation.15 | async-start | bytes 10485760 | tf_op jit(solution)/shard_map/reduce_scatter | solution.py:161
  497.6 114.3 %all-gather.11.cloned.1.call-start = ((), (), s32[]{:S(2)}) async-start(), calls=%async_computation.16 | async-start | bytes 5242880 | tf_op jit(solution)/shard_map/all_gather | solution.py:179
  577.2 351.4 %reduce-scatter.17.cloned.1.call-start = ((), (), s32[]{:S(2)}) async-start(), calls=%async_computation.17 | async-start | bytes 10485760 | tf_op jit(solution)/shard_map/reduce_scatter | solution.py:218
  808.4 161.2 %reduce-scatter.13.cloned.1.call-start = ((), (), s32[]{:S(2)}) async-start(), calls=%async_computation.13 | async-start | bytes 5242880 | tf_op jit(solution)/shard_map/reduce_scatter | solution.py:136
  819.6 197.3 %all-reduce.111.cloned.1.call-start = ((), (), s32[]{:S(2)}) async-start(), calls=%async_computation.24 | async-start | bytes 2621440 | tf_op jit(solution)/shard_map/psum | solution.py:245
  825.1 402.9 %reduce-scatter.25.cloned.1.call-start = ((), (), s32[]{:S(2)}) async-start(), calls=%async_computation.21 | async-start | bytes 14155776 | tf_op jit(solution)/shard_map/reduce_scatter | solution.py:268
  837.6 601.3 %reduce-scatter.27.cloned.1.call-start = ((), (), s32[]{:S(2)}) async-start(), calls=%async_computation.22 | async-start | bytes 14155776 | tf_op jit(solution)/shard_map/reduce_scatter | solution.py:269
  850.2 800.1 %reduce-scatter.29.cloned.1.call-start = ((), (), s32[]{:S(2)}) async-start(), calls=%async_computation.23 | async-start | bytes 14155776 | tf_op jit(solution)/shard_map/reduce_scatter | solution.py:270
  863.0 893.6 %reduce-scatter.21.cloned.1.call-start = ((), (), s32[]{:S(2)}) async-start(), calls=%async_computation.19 | async-start | bytes 5898240 | tf_op jit(solution)/shard_map/reduce_scatter | solution.py:266
  872.3 991.4 %reduce-scatter.23.cloned.1.call-start = ((), (), s32[]{:S(2)}) async-start(), calls=%async_computation.20 | async-start | bytes 5898240 | tf_op jit(solution)/shard_map/reduce_scatter | solution.py:267
  881.1 1089.4 %reduce-scatter.19.cloned.1.call-start = ((), (), s32[]{:S(2)}) async-start(), calls=%async_computation.18 | async-start | bytes 5898240 | tf_op jit(solution)/shard_map/reduce_scatter | solution.py:265
  890.6 79.0 %copy-start.159 = (f32[256]{0:T(256)S(1)}, f32[256]{0:T(256)}, u32[]{:S(2)}) copy-start(f32[256]{0:T(256)} %copy-done.158) | copy-start | bytes 3076
  890.6 79.1 %copy-start.99 = (f32[2048]{0:T(1024)S(1)}, f32[2048]{0:T(1024)}, u32[]{:S(2)}) copy-start(f32[2048]{0:T(1024)} %param.31) | copy-start | bytes 24580
  890.6 79.1 %copy-start.142 = (f32[256]{0:T(256)S(1)}, f32[256]{0:T(256)}, u32[]{:S(2)}) copy-start(f32[256]{0:T(256)} %copy-done.141) | copy-start | bytes 3076
  890.6 79.1 %copy-start.157 = (f32[256]{0:T(256)S(1)}, f32[256]{0:T(256)}, u32[]{:S(2)}) copy-start(f32[256]{0:T(256)} %copy-done.156) | copy-start | bytes 3076
  969.7 1004.8 %copy-start.1 = (bf16[640,2048]{1,0:T(8,128)(2,1)S(1)}, bf16[640,2048]{1,0:T(8,128)(2,1)}, u32[]{:S(2)}) copy-start(bf16[640,2048]{1,0:T(8,128)(2,1)} %param.30) | copy-start | bytes 7864324
  (154 other events, 1180.8 us)
Sparse Core Ops, SparseCore 0:
  12.2 37.1 all-gather.4
  310.2 71.7 reduce-scatter.10
  386.9 34.4 all-gather.6
  422.9 34.4 all-gather.8
  497.7 71.6 reduce-scatter.14
  577.4 34.4 all-gather.10
  808.5 71.7 reduce-scatter.16
  883.0 44.5 reduce-scatter.12
  932.3 84.5 all-reduce.110
  1021.4 206.5 reduce-scatter.24
  1232.5 206.4 reduce-scatter.26
  1443.4 206.8 reduce-scatter.28
  1654.9 101.6 reduce-scatter.20
  1761.0 102.7 reduce-scatter.22
  1868.2 102.2 reduce-scatter.18
where the time goes:
time: 2000 us; the launch traced here: 1980 us
  waiting for transfers between devices  1260 us (63%)
  local copies, waits for them, and re-layouts  314 us (16%)
  matrix products  186 us (9%)
  other arithmetic  130 us (6%)
  blocking collectives  76.6 us (4%)
    reduce_scatter x1, waiting for transfers between devices, on_device(): lax.psum_scatter(down_weight_gradient, 'dp', scatter_dimension=1, tiled=T...  211 us
    reduce_scatter x1, waiting for transfers between devices, on_device(): lax.psum_scatter(up_weight_gradient, 'dp', scatter_dimension=0, tiled=True)  211 us
    reduce_scatter x1, waiting for transfers between devices, on_device(): lax.psum_scatter(gate_weight_gradient, 'dp', scatter_dimension=0, tiled=T...  211 us
    slice x78, local copies, waits for them, and re-layouts, recurrence(): _, states = lax.associative_scan(combine_pairs, (carried, driven), axis=1)  158 us
    pad x79, local copies, waits for them, and re-layouts, recurrence(): _, states = lax.associative_scan(combine_pairs, (carried, driven), axis=1)  117 us
    reduce_scatter x1, waiting for transfers between devices, on_device(): lax.psum_scatter(output_weight_gradient, 'dp', scatter_dimension=1, tiled...  107 us
    reduce_scatter x1, waiting for transfers between devices, on_device(): lax.psum_scatter(gated_weight_gradient, 'dp', scatter_dimension=0, tiled=...  107 us
    reduce_scatter x1, waiting for transfers between devices, on_device(): lax.psum_scatter(grad_branch, 'dp', scatter_dimension=0, tiled=True)  106 us
  transfers between devices with their start and end apart: 15, of which 13 were waited for; matrix products, arithmetic and copies ran while one was open for 5% of the time, Pallas kernels for 0%

commit v1 on v0

v1 whole, which is shorter than its diff:
```python
import functools

import jax
import jax.numpy as jnp
from jax import lax
from jax.experimental import pallas as pl
from jax.experimental.pallas import tpu as pltpu
from jax.sharding import PartitionSpec as P

epsilon = 1e-06
decay_scale = 8.0
LANES = 128
GELU_C = 0.7978845608028654
GELU_K = 0.044715
F32 = jnp.float32
BF16 = jnp.bfloat16
VMEM_BYTES = 60 * 1024 * 1024


def minus_expm1(y, exp_y):
    s = 1.0 + y * (1.0 / 9.0)
    for d in range(8, 1, -1):
        s = 1.0 + (y * (1.0 / d)) * s
    return jnp.where(y > -0.5, -y * s, 1.0 - exp_y)


def gelu_parts(v):
    v2 = v * v
    t = jnp.tanh(GELU_C * v * (1.0 + GELU_K * v2))
    half = 0.5 * (1.0 + t)
    slope = half + 0.5 * v * (1.0 - t * t) * (GELU_C * (1.0 + 3.0 * GELU_K * v2))
    return v * half, slope


def lane_tiles(width):
    return [slice(j * LANES, (j + 1) * LANES) for j in range(width // LANES)]


def fold_rows(v):
    return jnp.sum(v.reshape(v.shape[0] // 8, 8, v.shape[1]), axis=0)


def gates_pre(rows, step, conv_ref, w_ref, pre_s):
    @pl.loop(0, rows // step)
    def _(i):
        r = pl.ds(pl.multiple_of(i * step, step), step)
        pre_s[r, :] = jnp.dot(conv_ref[r, :], w_ref[...], preferred_element_type=F32)


def mixer_forward_kernel(branch_ref, gated_ref, mask_ref, vec_ref, w_ref, conv_ref, states_ref, product_ref, pre_s, a_s, b_s):
    rows, width = branch_ref.shape
    seg = rows // 8
    tiles = lane_tiles(width)

    @pl.loop(0, 8)
    def _(s):
        t0 = pl.multiple_of(s * seg, seg)
        before = pl.multiple_of(jnp.maximum(t0 - 8, 0), 8)
        same = [mask_ref[pl.ds(t0, seg), k : k + 1] for k in range(3)]
        for cols in tiles:
            b = branch_ref[pl.ds(t0, seg), cols]
            ext = jnp.concatenate([branch_ref[pl.ds(before, 8), cols], b], axis=0)
            out = vec_ref[4:5, cols] + vec_ref[0:1, cols] * b
            for k in range(1, 4):
                out = out + vec_ref[k : k + 1, cols] * pltpu.roll(ext, k, 0)[8:] * same[k - 1]
            conv_ref[pl.ds(t0, seg), cols] = out.astype(BF16)

    gates_pre(rows, 256, conv_ref, w_ref, pre_s)

    @pl.loop(0, 8)
    def _(s):
        t0 = pl.multiple_of(s * seg, seg)
        c = mask_ref[pl.ds(t0, seg), 0:1]
        for j, cols in enumerate(tiles):
            cols_i = slice(width + j * LANES, width + (j + 1) * LANES)
            r = jax.nn.sigmoid(pre_s[pl.ds(t0, seg), cols] + vec_ref[5:6, cols])
            i = jax.nn.sigmoid(pre_s[pl.ds(t0, seg), cols_i] + vec_ref[6:7, cols])
            log_a = (-decay_scale * vec_ref[7:8, cols]) * r
            a = jnp.exp(log_a)
            n = jnp.sqrt(minus_expm1(2.0 * log_a, a * a))
            mult = (1.0 - c) + c * n
            a_s[j, pl.ds(t0, seg), :] = a * c
            b_s[j, pl.ds(t0, seg), :] = mult * i * conv_ref[pl.ds(t0, seg), cols].astype(F32)

    def scan_step(i, carry):
        out = []
        for j in range(len(tiles)):
            h, p = carry[j]
            at = pl.ds(i, 8, stride=seg)
            a = a_s[j, at, :]
            h = a * h + b_s[j, at, :]
            p = a * p
            b_s[j, at, :] = h
            a_s[j, at, :] = p
            out.append((h, p))
        return tuple(out)

    one = jnp.ones((8, LANES), F32)
    lax.fori_loop(0, seg, scan_step, tuple((jnp.zeros((8, LANES), F32), one) for _ in tiles), unroll=4)

    def finish(s, carry):
        t0 = pl.multiple_of(s * seg, seg)
        out = []
        for j, cols in enumerate(tiles):
            st = b_s[j, pl.ds(t0, seg), :] + a_s[j, pl.ds(t0, seg), :] * carry[j]
            states_ref[pl.ds(t0, seg), cols] = st
            act, _ = gelu_parts(gated_ref[pl.ds(t0, seg), cols])
            product_ref[pl.ds(t0, seg), cols] = (st * act).astype(BF16)
            out.append(st[seg - 1 : seg, :])
        return tuple(out)

    lax.fori_loop(0, 8, finish, tuple(jnp.zeros((1, LANES), F32) for _ in tiles))


def mixer_forward(branch_pre, gated_pre, masks, vecs, w_cat):
    rows, width = branch_pre.shape
    lanes = width // LANES
    return pl.pallas_call(
        mixer_forward_kernel,
        out_shape=[
            jax.ShapeDtypeStruct((rows, width), BF16),
            jax.ShapeDtypeStruct((rows, width), F32),
            jax.ShapeDtypeStruct((rows, width), BF16),
        ],
        scratch_shapes=[
            pltpu.VMEM((rows, 2 * width), F32),
            pltpu.VMEM((lanes, rows, LANES), F32),
            pltpu.VMEM((lanes, rows, LANES), F32),
        ],
        compiler_params=pltpu.CompilerParams(vmem_limit_bytes=VMEM_BYTES),
        cost_estimate=pl.CostEstimate(flops=4 * rows * width * width, bytes_accessed=rows * width * 16, transcendentals=6 * rows * width),
        name="mixer_forward",
    )(branch_pre, gated_pre, masks, vecs, w_cat)


def mixer_backward_kernel(
    dprod_ref, gated_ref, states_ref, branch_ref, conv_ref, mask_ref, vec_ref, w_ref,
    dgated_ref, dri_ref, dbranch_ref, sums_ref,
    pre_s, a_s, n_s, ac_s, e_s, p_s, dconv_s,
):
    rows, width = branch_ref.shape
    seg = rows // 8
    tiles = lane_tiles(width)
    sums_ref[...] = jnp.zeros_like(sums_ref)
    gates_pre(rows, 256, conv_ref, w_ref, pre_s)

    @pl.loop(0, 8)
    def _(s):
        t0 = pl.multiple_of(s * seg, seg)
        at = pl.ds(t0, seg)
        c = mask_ref[at, 0:1]
        for j, cols in enumerate(tiles):
            cols_i = slice(width + j * LANES, width + (j + 1) * LANES)
            r = jax.nn.sigmoid(pre_s[at, cols] + vec_ref[5:6, cols])
            pre_s[at, cols] = r
            pre_s[at, cols_i] = jax.nn.sigmoid(pre_s[at, cols_i] + vec_ref[6:7, cols])
            log_a = (-decay_scale * vec_ref[7:8, cols]) * r
            a = jnp.exp(log_a)
            a_s[at, cols] = a
            n_s[at, cols] = jnp.sqrt(minus_expm1(2.0 * log_a, a * a))
            ac_s[j, at, :] = a * c
            act, slope = gelu_parts(gated_ref[at, cols])
            d = dprod_ref[at, cols]
            e_s[j, at, :] = d * act
            dgated_ref[at, cols] = (d * states_ref[at, cols] * slope).astype(BF16)

    for j in range(len(tiles)):
        ac_s[j, rows : rows + 8, :] = jnp.zeros((8, LANES), F32)

    def scan_step(q, carry):
        i = seg - 1 - q
        out = []
        for j in range(len(tiles)):
            e, p = carry[j]
            at = pl.ds(i, 8, stride=seg)
            a = ac_s[j, pl.ds(i + 1, 8, stride=seg), :]
            e = a * e + e_s[j, at, :]
            p = a * p
            e_s[j, at, :] = e
            p_s[j, at, :] = p
            out.append((e, p))
        return tuple(out)

    one = jnp.ones((8, LANES), F32)
    lax.fori_loop(0, seg, scan_step, tuple((jnp.zeros((8, LANES), F32), one) for _ in tiles), unroll=4)

    def finish(q, carry):
        s = 7 - q
        t0 = pl.multiple_of(s * seg, seg)
        at = pl.ds(t0, seg)
        before = pl.multiple_of(jnp.maximum(t0 - 8, 0), 8)
        c = mask_ref[at, 0:1]
        out = []
        for j, cols in enumerate(tiles):
            cols_i = slice(width + j * LANES, width + (j + 1) * LANES)
            e = e_s[j, at, :] + p_s[j, at, :] * carry[j]
            out.append(e[0:1, :])
            ext = jnp.concatenate([states_ref[pl.ds(before, 8), cols], states_ref[at, cols]], axis=0)
            earlier = pltpu.roll(ext, 1, 0)[8:]
            r, i, a, n = pre_s[at, cols], pre_s[at, cols_i], a_s[at, cols], n_s[at, cols]
            cv = conv_ref[at, cols].astype(F32)
            ec = e * c
            d_log = a * (ec * earlier) - ec * i * cv * (a * a / n)
            rr = d_log * r
            dr = ((-decay_scale * vec_ref[7:8, cols]) * rr * (1.0 - r)).astype(BF16)
            em = e * ((1.0 - c) + c * n) * i
            di = (em * cv * (1.0 - i)).astype(BF16)
            dri_ref[at, cols] = dr
            dri_ref[at, cols_i] = di
            dconv_s[at, cols] = em
            sums_ref[5, :, cols] += fold_rows(dr.astype(F32))
            sums_ref[6, :, cols] += fold_rows(di.astype(F32))
            sums_ref[7, :, cols] += fold_rows(rr)
        return tuple(out)

    lax.fori_loop(0, 8, finish, tuple(jnp.zeros((1, LANES), F32) for _ in tiles))

    @pl.loop(0, rows // 256)
    def _(i):
        at = pl.ds(pl.multiple_of(i * 256, 256), 256)
        dconv_s[at, :] += lax.dot_general(dri_ref[at, :], w_ref[...], (((1,), (1,)), ((), ())), preferred_element_type=F32)

    dconv_s[rows : rows + 8, :] = jnp.zeros((8, width), F32)

    @pl.loop(0, 8)
    def _(s):
        t0 = pl.multiple_of(s * seg, seg)
        at, ext = pl.ds(t0, seg), pl.ds(t0, seg + 8)
        same = [mask_ref[ext, k : k + 1] for k in range(3)]
        for cols in tiles:
            d = dconv_s[ext, cols]
            b = branch_ref[at, cols]
            sums_ref[4, :, cols] += fold_rows(d[:seg])
            sums_ref[0, :, cols] += fold_rows(d[:seg] * b)
            total = vec_ref[0:1, cols] * d[:seg]
            for k in range(1, 4):
                moved = pltpu.roll(d * same[k - 1], seg + 8 - k, 0)[:seg]
                total = total + vec_ref[k : k + 1, cols] * moved
                sums_ref[k, :, cols] += fold_rows(moved * b)
            dbranch_ref[at, cols] = total.astype(BF16)


def mixer_backward(d_product, gated_pre, states, branch_pre, conv_out, masks, vecs, w_cat):
    rows, width = branch_pre.shape
    lanes = width // LANES
    return pl.pallas_call(
        mixer_backward_kernel,
        out_shape=[
            jax.ShapeDtypeStruct((rows, width), BF16),
            jax.ShapeDtypeStruct((rows, 2 * width), BF16),
            jax.ShapeDtypeStruct((rows, width), BF16),
            jax.ShapeDtypeStruct((8, 8, width), F32),
        ],
        scratch_shapes=[
            pltpu.VMEM((rows, 2 * width), F32),
            pltpu.VMEM((rows, width), F32),
            pltpu.VMEM((rows, width), F32),
            pltpu.VMEM((lanes, rows + 8, LANES), F32),
            pltpu.VMEM((lanes, rows, LANES), F32),
            pltpu.VMEM((lanes, rows, LANES), F32),
            pltpu.VMEM((rows + 8, width), F32),
        ],
        compiler_params=pltpu.CompilerParams(vmem_limit_bytes=VMEM_BYTES),
        cost_estimate=pl.CostEstimate(flops=8 * rows * width * width, bytes_accessed=rows * width * 26, transcendentals=8 * rows * width),
        name="mixer_backward",
    )(d_product, gated_pre, states, branch_pre, conv_out, masks, vecs, w_cat)


class Stage:
    def __init__(self, stride, size, later):
        self.stride, self.size, self.later = stride, size, later
        self.blocks = 1
        for s in later:
            self.blocks *= s.size
        self.digit = lax.rem(lax.axis_index("dp") // stride, size)

    def offset(self, position):
        total = 0
        for s in reversed(self.later):
            total = total + lax.rem(position, s.size) * s.stride
            position = position // s.size
        return total


def digit_sizes(n):
    if n == 8:
        return [2, 4]
    sizes = []
    while n > 1:
        m = 4 if n % 4 == 0 else 2 if n % 2 == 0 else n
        sizes.append(m)
        n //= m
    return sizes


def make_stages(n, last_first):
    digits, stride = [], 1
    for m in digit_sizes(n):
        digits.append((stride, m))
        stride *= m
    if last_first:
        digits = digits[1:] + digits[:1]
    stages = []
    for stride, m in reversed(digits):
        stages.insert(0, Stage(stride, m, list(stages)))
    return stages


class Item:
    def __init__(self, number, stages, left, right, width, refs):
        self.number, self.stages, self.left, self.right, self.width = number, stages, left, right, width
        self.columns = right.shape[1]
        self.out, self.recv, self.send, self.send_sem, self.recv_sem = refs

    def message(self, t, back, k, slot):
        stage = self.stages[t]
        step = jnp.where(back, -stage.stride, stage.stride)
        return pltpu.make_async_remote_copy(
            src_ref=self.send[t].at[slot],
            dst_ref=self.recv[t].at[back, k - 1],
            send_sem=self.send_sem[t].at[slot],
            recv_sem=self.recv_sem[t].at[back, k - 1],
            device_id={"dp": lax.axis_index("dp") + step},
            device_id_type=pl.DeviceIdType.MESH,
        )


class Engine:
    def __init__(self, left_s, got_s, sem):
        self.left_s, self.got_s, self.sem = left_s, got_s, sem

    def fetch_left(self, item, block):
        source = item.left.at[block] if len(item.left.shape) == 3 else item.left.at[:, pl.ds(pl.multiple_of(block * item.width, item.width), item.width)]
        return pltpu.make_async_copy(source, self.left_s, self.sem.at[0])

    def product(self, item, block, gots, store):
        fetch = self.fetch_left(item, block)
        fetch.start()
        views = []
        for i, (condition, source) in enumerate(gots):
            view = self.got_s.at[i, :, pl.ds(0, item.columns)]
            views.append(view)

            @pl.when(condition)
            def _(view=view, source=source, i=i):
                pltpu.make_async_copy(source, view, self.sem.at[1 + i]).start()

        for i, (condition, source) in enumerate(gots):

            @pl.when(condition)
            def _(view=views[i], source=source, i=i):
                pltpu.make_async_copy(source, view, self.sem.at[1 + i]).wait()

        fetch.wait()
        tile = 512 if item.columns % 512 == 0 else item.columns
        for c in range(item.columns // tile):
            cols = pl.ds(c * tile, tile)
            total = lax.dot_general(self.left_s[...], item.right[:, cols], (((0,), (0,)), ((), ())), preferred_element_type=F32)
            for (condition, _), view in zip(gots, views):
                total = total + jnp.where(condition, view[:, cols].astype(F32), 0.0)
            store(cols, total)

    def arrived(self, item, t, position):
        found = []
        for u in range(t):
            stage = item.stages[u]
            spot = position
            rows = None
            scale = 1
            for s in item.stages[t:]:
                scale *= s.size
            lead = 0
            for s in item.stages[u + 1 : t]:
                lead = lead * s.size + s.digit
            rows = pl.ds((lead * scale + spot) * item.width, item.width)
            last = stage.size - 2
            if stage.size == 2:
                back = jnp.where(stage.digit == 0, 1, 0)
                found.append((stage.digit >= 0, item.recv[u].at[back, last, rows]))
            else:
                found.append((stage.digit >= 1, item.recv[u].at[0, last, rows]))
                found.append((stage.digit <= stage.size - 2, item.recv[u].at[1, last, rows]))
        return found

    def own_base(self, item, t):
        base = 0
        for s in item.stages[:t]:
            base = base + s.digit * s.stride
        return base

    def wait_last(self, item, t):
        stage = item.stages[t]
        for back in range(2):
            me = stage.digit if back == 0 else stage.size - 1 - stage.digit

            @pl.when(me >= 1)
            def _(back=back):
                item.message(t, back, stage.size - 1, 0).wait_recv()

    def round(self, item, t, k):
        stage = item.stages[t]
        if k == 1 and t > 0:
            self.wait_last(item, t - 1)
        base = self.own_base(item, t)

        @pl.loop(0, 2)
        def _(back):
            me = jnp.where(back == 0, stage.digit, stage.size - 1 - stage.digit)

            @pl.when(me <= k - 1)
            def _():
                there = me + stage.size - k
                value = jnp.where(back == 0, there, stage.size - 1 - there)
                slot = jnp.where(value > stage.digit, value - 1, value)
                if k > 1:

                    @pl.when(me >= 1)
                    def _():
                        item.message(t, back, k - 1, 0).wait_recv()

                @pl.loop(0, stage.blocks)
                def _(p):
                    block = base + value * stage.stride + stage.offset(p)
                    rows = pl.ds(p * item.width, item.width)
                    gots = self.arrived(item, t, value * stage.blocks + p)
                    if k > 1:
                        gots.append((me >= 1, item.recv[t].at[back, k - 2, rows]))

                    def store(cols, total):
                        item.send[t][slot, rows, cols] = total.astype(BF16)

                    self.product(item, block, gots, store)

                item.message(t, back, k, slot).start()

    def finish(self, item, out_s):
        t = len(item.stages)
        self.wait_last(item, t - 1)

        def store(cols, total):
            out_s[:, cols] = total

        self.product(item, self.own_base(item, t), self.arrived(item, t, 0), store)
        copy = pltpu.make_async_copy(out_s.at[:, pl.ds(0, item.columns)], item.out, self.sem.at[0])
        copy.start()
        copy.wait()

    def drain(self, item):
        for t, stage in enumerate(item.stages):
            for slot in range(stage.size - 1):
                item.message(t, 0, 1, slot).wait_send()


def dp_scatter_kernel(plan, order, lefts_of, widths, *refs):
    count = len(plan)
    n_left = max(lefts_of) + 1
    lefts, refs = refs[:n_left], refs[n_left:]
    rights_hbm, refs = refs[:count], refs[count:]
    outs, refs = refs[:count], refs[count:]
    all_stages = [make_stages(lax.axis_size("dp"), last_first) for last_first in plan]
    recv, sends, send_sems, recv_sems = [], [], [], []
    for stages in all_stages:
        recv.append(refs[: len(stages)])
        refs = refs[len(stages) :]
    rights, refs = refs[:count], refs[count:]
    for stages in all_stages:
        sends.append(refs[: len(stages)])
        refs = refs[len(stages) :]
    for stages in all_stages:
        send_sems.append(refs[: len(stages)])
        recv_sems.append(refs[len(stages) : 2 * len(stages)])
        refs = refs[2 * len(stages) :]
    left_s, got_s, out_s, right_sem, sem = refs
    loads = [pltpu.make_async_copy(rights_hbm[i], rights[i], right_sem.at[i]) for i in range(count)]
    for load in loads:
        load.start()
    items = [
        Item(i, all_stages[i], lefts[lefts_of[i]], rights[i], widths, (outs[i], recv[i], sends[i], send_sems[i], recv_sems[i]))
        for i in range(count)
    ]
    engine = Engine(left_s, got_s, sem)
    loaded = set()
    for i, t, k in order:
        if i not in loaded:
            loads[i].wait()
            loaded.add(i)
        if t < len(all_stages[i]):
            engine.round(items[i], t, k)
        else:
            engine.finish(items[i], out_s)
    for item in items:
        engine.drain(item)


def task_order(plan, names, n):
    tasks = []
    for i, last_first in enumerate(plan):
        sizes = digit_sizes(n)
        if last_first:
            sizes = sizes[1:] + sizes[:1]
        tasks.append([(i, t, k) for t, m in enumerate(sizes) for k in range(1, m)] + [(i, len(sizes), 0)])
    out, at = [], [0] * len(plan)
    for i in names:
        if at[i] < len(tasks[i]):
            out.append(tasks[i][at[i]])
            at[i] += 1
    for i in range(len(plan)):
        out += tasks[i][at[i] :]
    return out


def dp_scatter(lefts, lefts_of, rights, plan, names):
    n = lax.axis_size("dp")
    tokens, features = lefts[0].shape
    width = features // n
    if width % LANES:
        lefts = [v.reshape(tokens, n, width).transpose(1, 0, 2) for v in lefts]
    widest = max(r.shape[1] for r in rights)
    hbm = pl.BlockSpec(memory_space=pl.ANY)
    out_shape = [jax.ShapeDtypeStruct((width, r.shape[1]), F32) for r in rights]
    send_shapes, semaphores = [], []
    for r, last_first in zip(rights, plan):
        sizes = digit_sizes(n)
        if last_first:
            sizes = sizes[1:] + sizes[:1]
        left_over, sends, recvs = n, [], []
        for m in sizes:
            left_over //= m
            out_shape.append(jax.ShapeDtypeStruct((2, m - 1, left_over * width, r.shape[1]), BF16))
            send_shapes.append(pltpu.VMEM((m - 1, left_over * width, r.shape[1]), BF16))
            sends.append(pltpu.SemaphoreType.DMA((m - 1,)))
            recvs.append(pltpu.SemaphoreType.DMA((2, m - 1)))
        semaphores += sends + recvs
    gots = 2 * len(digit_sizes(n))
    scratch = [pltpu.VMEM(r.shape, BF16) for r in rights] + send_shapes + semaphores
    scratch += [
        pltpu.VMEM((tokens, width), BF16),
        pltpu.VMEM((gots, width, widest), BF16),
        pltpu.VMEM((width, widest), F32),
        pltpu.SemaphoreType.DMA((len(rights),)),
        pltpu.SemaphoreType.DMA((1 + gots,)),
    ]
    columns = sum(r.shape[1] for r in rights)
    results = pl.pallas_call(
        functools.partial(dp_scatter_kernel, plan, task_order(plan, names, n), lefts_of, width),
        out_shape=out_shape,
        in_specs=[hbm] * (len(lefts) + len(rights)),
        out_specs=[hbm] * len(out_shape),
        scratch_shapes=scratch,
        compiler_params=pltpu.CompilerParams(vmem_limit_bytes=VMEM_BYTES, has_side_effects=True),
        cost_estimate=pl.CostEstimate(flops=2 * tokens * features * columns, bytes_accessed=4 * features * columns, transcendentals=0),
        name="dp_scatter",
    )(*lefts, *rights)
    return results[: len(rights)]

DP_PLAN = [True, False, False, False, False, False]
DP_ORDER = [0, 1, 2, 0, 1, 0, 1, 3, 4, 5, 1, 0, 1, 2, 2, 0, 2, 2, 3, 3, 3, 3, 4, 4, 4, 4, 5, 5, 5, 5]


def rms_stats(values):
    return lax.rsqrt(jnp.mean(values * values, axis=-1, keepdims=True) + epsilon)


def rms_back(values, inverse, gain, d_normed):
    weighted = gain * d_normed
    inner = jnp.mean(weighted * values, axis=-1, keepdims=True)
    d_values = inverse * weighted - values * (inverse * inverse * inverse * inner)
    return d_values, jnp.sum(d_normed * values * inverse, axis=0)


def dot(left, right, dims, out=F32):
    return lax.dot_general(left, right, (dims, ((), ())), preferred_element_type=F32).astype(out)


def spread_heads(weight):
    heads, width = weight.shape[:2]
    eye = jnp.eye(heads, dtype=weight.dtype)
    return (weight[:, :, None, :] * eye[:, None, :, None]).reshape(heads * width, heads * width)


def head_blocks(dense, heads, width):
    return jnp.stack([dense[h * width : (h + 1) * width, h * width : (h + 1) * width] for h in range(heads)])


def on_device(
    stream_in, segments, first_gain, gelu_gate_weight, recurrent_branch_weight, conv_kernel, conv_bias, recur_weight, recur_bias,
    inlet_weight, inlet_bias, decay_param, recurrent_output_weight, second_gain, gate_projection_weight, up_projection_weight,
    down_projection_weight, cotangent,
):
    values = stream_in[0].astype(F32)
    seq_len = segments.shape[1]
    heads, head_width = recur_weight.shape[:2]
    gather = lambda v: lax.all_gather(v, "tensor", axis=0, tiled=True)
    reduce = lambda v: lax.psum_scatter(v, "tensor", scatter_dimension=0, tiled=True).astype(F32)

    ids = jnp.pad(segments[0], (3, 8), constant_values=-1)
    same = [(ids[3 - k : 3 - k + seq_len] == segments[0]).astype(F32) for k in range(1, 4)]
    masks = jnp.pad(jnp.stack(same, axis=1), ((0, 8), (0, 5)))
    softplus = jax.nn.softplus(-decay_param)
    vecs = jnp.concatenate([conv_kernel, jnp.stack([conv_bias, recur_bias, inlet_bias, softplus])])
    w_cat = jnp.concatenate([spread_heads(recur_weight), spread_heads(inlet_weight)], axis=1)

    first_inverse = rms_stats(values)
    normed = gather((values * first_inverse * first_gain).astype(BF16))
    cot = gather(cotangent[0])
    gated_pre = dot(normed, gelu_gate_weight, ((1,), (0,)))
    branch_pre = dot(normed, recurrent_branch_weight, ((1,), (0,)))
    conv_out, states, product = mixer_forward(branch_pre, gated_pre, masks, vecs, w_cat)
    attended = reduce(dot(product, recurrent_output_weight, ((1,), (0,)), BF16))
    middle = values + attended
    second_inverse = rms_stats(middle)
    normed_two = gather((middle * second_inverse * second_gain).astype(BF16))
    gate_pre = dot(normed_two, gate_projection_weight, ((1,), (0,)))
    up_pre = dot(normed_two, up_projection_weight, ((1,), (0,)))
    gate_act, gate_slope = gelu_parts(gate_pre)
    hidden = (gate_act * up_pre).astype(BF16)
    d_hidden = dot(cot, down_projection_weight, ((1,), (1,)))
    d_gate = (d_hidden * up_pre * gate_slope).astype(BF16)
    d_up = (d_hidden * gate_act).astype(BF16)
    d_normed_two = reduce(
        (dot(d_gate, gate_projection_weight, ((1,), (1,))) + dot(d_up, up_projection_weight, ((1,), (1,)))).astype(BF16)
    )
    ffn_out = reduce(dot(hidden, down_projection_weight, ((1,), (0,)), BF16))
    stream_out = middle + ffn_out
    d_middle, grad_second = rms_back(middle, second_inverse, second_gain, d_normed_two)
    d_middle = cotangent[0].astype(F32) + d_middle
    d_attended = gather(d_middle.astype(BF16))
    d_product = dot(d_attended, recurrent_output_weight, ((1,), (1,)))
    d_gated, d_ri, d_branch, sums = mixer_backward(
        d_product, gated_pre, states, branch_pre, conv_out, masks, vecs, w_cat
    )
    d_normed = reduce(
        (dot(d_gated, gelu_gate_weight, ((1,), (1,))) + dot(d_branch, recurrent_branch_weight, ((1,), (1,)))).astype(BF16)
    )
    d_values, grad_first = rms_back(values, first_inverse, first_gain, d_normed)
    stream_grad = d_middle + d_values

    down_gradient, gate_gradient, up_gradient, output_gradient, gated_gradient, branch_gradient = dp_scatter(
        [cot, normed_two, d_attended, normed],
        [0, 1, 1, 2, 3, 3],
        [hidden, d_gate, d_up, product, d_gated, d_branch],
        DP_PLAN,
        DP_ORDER,
    )

    width = heads * head_width
    dense = dot(conv_out, d_ri, ((0,), (0,)))
    grad_recur = head_blocks(dense[:, :width], heads, head_width)
    grad_inlet = head_blocks(dense[:, width:], heads, head_width)
    sums = jnp.sum(sums, axis=1)
    small = jnp.concatenate([sums.reshape(-1), grad_recur.reshape(-1), grad_inlet.reshape(-1)])
    small = lax.psum(small, "dp")
    sums = small[: 8 * width].reshape(8, width)
    grad_recur, grad_inlet = small[8 * width :].reshape(2, heads, head_width, head_width)
    grad_decay = decay_scale * jax.nn.sigmoid(-decay_param) * sums[7]
    gains = lax.psum(jnp.concatenate([grad_first, grad_second]), ("dp", "tensor"))
    model = grad_first.shape[0]
    return (
        stream_out[None], stream_grad[None], gains[:model], gated_gradient, branch_gradient, sums[:4], sums[4], grad_recur, sums[5],
        grad_inlet, sums[6], grad_decay, output_gradient.T, gains[model:], gate_gradient, up_gradient, down_gradient.T,
    )


def solution(mesh):
    in_specs = (
        P("dp", "tensor", None),
        P("dp", None),
        P(),
        P(None, "tensor"),
        P(None, "tensor"),
        P(None, "tensor"),
        P("tensor"),
        P("tensor", None, None),
        P("tensor"),
        P("tensor", None, None),
        P("tensor"),
        P("tensor"),
        P("tensor", None),
        P(),
        P(None, "tensor"),
        P(None, "tensor"),
        P("tensor", None),
        P("dp", "tensor", None),
    )
    out_specs = (
        P("dp", "tensor", None),
        P("dp", "tensor", None),
        P(),
        P("dp", "tensor"),
        P("dp", "tensor"),
        P(None, "tensor"),
        P("tensor"),
        P("tensor", None, None),
        P("tensor"),
        P("tensor", None, None),
        P("tensor"),
        P("tensor"),
        P("tensor", "dp"),
        P(),
        P("dp", "tensor"),
        P("dp", "tensor"),
        P("tensor", "dp"),
    )
    return jax.shard_map(
        on_device, mesh=mesh, in_specs=in_specs, out_specs=out_specs, check_vma=False
    )
```

time: 2000 us -> 880 us (0.44)
  waiting for transfers between devices: 1260 us -> 195 us
  Pallas kernels: 0 us -> 444 us
  local copies, waits for them, and re-layouts: 314 us -> 25 us
  other arithmetic: 130 us -> 27.4 us
  matrix products: 186 us -> 127 us
  blocking collectives: 76.6 us -> 41.6 us
    reduce_scatter x10 -> x4, waiting for transfers between devices: 1100 us -> 89 us  [on_device(): lax.psum_scatter(v, 'tensor', scatter_dimension=0, tiled=True).astype(F32)]
    pallas_call x0 -> x3, Pallas kernels: none -> 444 us  [the longest x1 383 us: dp_scatter(): pl.pallas_call(functools.partial(dp_scatter_kernel, plan, task_order(plan...]
    slice x79 -> x4, local copies, waits for them, and re-layouts: 158 us -> 1.22 us  [the longest x3 0.61 us: on_device(): sums[:4]]
    pad x79 -> x0, local copies, waits for them, and re-layouts: 117 us -> none  [recurrence(): _, states = lax.associative_scan(combine_pairs, (carried, driven), axis=1)]
    dot_general x24 -> x13, matrix products: 186 us -> 127 us  [dot(): lax.dot_general(left, right, (dims, ((), ())), preferred_element_type=F32)]
    psum x1, waiting for transfers between devices: 40.3 us -> 0.01 us  [on_device(): small = lax.psum(small, 'dp')]
    psum x2 -> x1, blocking collectives: 76.6 us -> 41.6 us  [on_device(): lax.psum(jnp.concatenate([grad_first, grad_second]), ('dp', 'tensor'))]
    mul x21 -> x4, other arithmetic: 30.8 us -> 4.31 us  [the longest x1 2.87 us: spread_heads(): weight[:, :, None, :] * eye[:, None, :, None]]
  transfers between devices with their start and end apart: 15 -> 9, of which waited for: 13 -> 6; matrix products, arithmetic and copies ran while one was open for 5% -> 8% of each run, Pallas kernels for 0% -> 44%
where the time goes in v1:
time: 880 us; the launch traced here: 876 us
  Pallas kernels  444 us (50%)
  waiting for transfers between devices  195 us (22%)
  matrix products  127 us (14%)
  blocking collectives  41.6 us (5%)
  other arithmetic  27.4 us (3%)
  local copies, waits for them, and re-layouts  25 us (3%)
  between operations  14.5 us (2%)
    pallas_call x1, Pallas kernels, dp_scatter(): pl.pallas_call(functools.partial(dp_scatter_kernel, plan, task_order(plan...  383 us
    dot_general x13, matrix products, dot(): lax.dot_general(left, right, (dims, ((), ())), preferred_element_type=F32)  127 us
    all_gather x4, waiting for transfers between devices, on_device(): gather = lambda v: lax.all_gather(v, 'tensor', axis=0, tiled=True)  105 us
    reduce_scatter x4, waiting for transfers between devices, on_device(): lax.psum_scatter(v, 'tensor', scatter_dimension=0, tiled=True).astype(F32)  89 us
    psum x1, blocking collectives, on_device(): lax.psum(jnp.concatenate([grad_first, grad_second]), ('dp', 'tensor'))  41.6 us
    pallas_call x1, Pallas kernels, mixer_backward(): pl.pallas_call(mixer_backward_kernel, out_shape=[jax.ShapeDtypeStruct((ro...  35.2 us
    pallas_call x1, Pallas kernels, mixer_forward(): pl.pallas_call(mixer_forward_kernel, out_shape=[jax.ShapeDtypeStruct((row...  25.8 us
  transfers between devices with their start and end apart: 9, of which 6 were waited for; matrix products, arithmetic and copies ran while one was open for 8% of the time, Pallas kernels for 44%

profile of v1, /device:TPU:0, one launch (start us, length us, event | category | flops | bytes accessed | tf_op | source)
XLA Modules:
  0.0 875.7 jit_solution(10155495205299708045)
XLA Ops:
  10.1 2.5 fusion.14
  13.7 2.9 broadcast_multiply_fusion
  18.7 2.8 mul.258
  23.2 2.2 constant_dynamic-update-slice_fusion.w_ref
  26.2 23.7 %all-gather.6.cloned.1.call-done.refs_3_ = bf16[1024,2048]{1,0:T(8,128)(2,1)} async-done(((bf16[256,2048]{1,0:T(8,128)(2,1)}), bf16[1024,2048]{1,0:T(8,128)(2,1)}) %all-gather.6.cloned.1.call-update) | async-done | bytes 4194320 | tf_op jit(solution)/shard_map/all_gather | solution.py:593
  49.9 8.1 fusion.29.branch_ref
  58.1 4.9 fusion.30.gated_ref
  63.0 25.8 %mixer_forward.1 = (bf16[1024,640]{1,0:T(8,128)(2,1)}, f32[1024,640]{1,0:T(8,128)}, bf16[1024,640]{1,0:T(8,128)(2,1)}) custom-call(f32[1024,640]{1,0:T(8,128)} %fusion.29.branch_ref, f32[1024,640]{1,0:T(8,128)} %fusion.30.gated_ref, f32[1032,8]{1,0:T(8,128)} %pad_convert_fusion.mask_ref, f32[8,640]{1,0:T(8,128)} %concatenate.12.vec_ref, ...), custom_call_target="tpu_custom_call" | custom-call | flops 1677721600 | bytes 10485760 | tf_op jit(solution)/shard_map/mixer_forward/pallas_call | solution.py:118
  88.8 6.3 convolution_convert_fusion.1
  95.4 44.4 %reduce-scatter.5.cloned.1.call-done = bf16[256,2048]{1,0:T(8,128)(2,1)} async-done(((bf16[1024,2048]{1,0:T(8,128)(2,1)}), bf16[256,2048]{1,0:T(8,128)(2,1)}) %reduce-scatter.5.cloned.1.call-update) | async-done | bytes 1048592 | tf_op jit(solution)/shard_map/reduce_scatter | solution.py:594
  139.8 2.1 multiply_reduce_fusion
  144.1 34.0 %all-gather.8.cloned.1.call-done.refs_1_ = bf16[1024,2048]{1,0:T(8,128)(2,1)} async-done(((bf16[256,2048]{1,0:T(8,128)(2,1)}), bf16[1024,2048]{1,0:T(8,128)(2,1)}) %all-gather.8.cloned.1.call-update) | async-done | bytes 4194320 | tf_op jit(solution)/shard_map/all_gather | solution.py:593
  178.1 12.6 %fusion.31 = f32[1024,1536]{1,0:T(8,128)} fusion(bf16[1024,2048]{1,0:T(8,128)(2,1)} %all-gather.8.cloned.1.call-done.refs_1_, bf16[2048,1536]{1,0:T(8,128)(2,1)} %param.32), kind=kOutput, calls=%fused_computation.80 | convolution fusion | flops 6442450944 | bytes 16777216 | tf_op jit(solution)/shard_map/dot_general | solution.py:572
  190.7 10.5 %fusion.32 = f32[1024,1536]{1,0:T(8,128)} fusion(bf16[1024,2048]{1,0:T(8,128)(2,1)S(1)} %copy-done.33, bf16[2048,1536]{1,0:T(8,128)(2,1)} %param.33), kind=kOutput, calls=%fused_computation.81 | convolution fusion | flops 6442450944 | bytes 16777216 | tf_op jit(solution)/shard_map/dot_general | solution.py:572
  201.1 13.0 %all-gather.12.cloned.1.call-done = bf16[1,1024,2048]{2,1,0:T(8,128)(2,1)} async-done(((bf16[1,256,2048]{2,1,0:T(8,128)(2,1)}), bf16[1,1024,2048]{2,1,0:T(8,128)(2,1)}) %all-gather.12.cloned.1.call-update) | async-done | bytes 4194320 | tf_op jit(solution)/shard_map/all_gather | solution.py:593
  214.1 17.4 %multiply_convert_fusion = (bf16[1024,1536]{1,0:T(8,128)(2,1)S(1)}, bf16[1024,1536]{1,0:T(8,128)(2,1)S(1)}, bf16[1024,1536]{1,0:T(8,128)(2,1)}) fusion(f32[1024,1536]{1,0:T(8,128)} %fusion.31, f32[1024,1536]{1,0:T(8,128)} %fusion.32, bf16[1536,2048]{1,0:T(8,128)(2,1)} %param.34, bf16[1,1024,2048]{2,1,0:T(8,128)(2,1)} %all-gather.12.cloned.1.call-done), kind=kOutput, calls=%fused_computation.2 | convolution fusion | flops 6480199680 | bytes 32505856 | tf_op jit(solution)/shard_map/dot_general | solution.py:572
  231.5 11.1 %fusion.33 = f32[1024,2048]{1,0:T(8,128)S(1)} fusion(bf16[1024,1536]{1,0:T(8,128)(2,1)S(1)} %get-tuple-element.99.refs_5_, bf16[2048,1536]{1,0:T(8,128)(2,1)} %param.32), kind=kOutput, calls=%fused_computation.82 | convolution fusion | flops 6442450944 | bytes 17825792 | tf_op jit(solution)/shard_map/dot_general | solution.py:572
  242.6 23.9 %add_convert_fusion.1 = bf16[1024,2048]{1,0:T(8,128)(2,1)} fusion(f32[1024,2048]{1,0:T(8,128)S(1)} %fusion.33, bf16[1024,1536]{1,0:T(8,128)(2,1)S(1)} %get-tuple-element.98.refs_6_, bf16[2048,1536]{1,0:T(8,128)(2,1)} %param.33), kind=kOutput, calls=%fused_computation.1 | convolution fusion | flops 6446645248 | bytes 22020096 | tf_op jit(solution)/shard_map/dot_general | solution.py:572
  266.6 44.6 %reduce-scatter.9.cloned.1.call-done = bf16[256,2048]{1,0:T(8,128)(2,1)} async-done(((bf16[1024,2048]{1,0:T(8,128)(2,1)}), bf16[256,2048]{1,0:T(8,128)(2,1)}) %reduce-scatter.9.cloned.1.call-update) | async-done | bytes 1048592 | tf_op jit(solution)/shard_map/reduce_scatter | solution.py:594
  311.2 2.7 fusion.11
  314.0 3.0 fusion.26
  317.1 34.6 %all-gather.10.cloned.1.call-done.refs_2_ = bf16[1024,2048]{1,0:T(8,128)(2,1)} async-done(((bf16[256,2048]{1,0:T(8,128)(2,1)}), bf16[1024,2048]{1,0:T(8,128)(2,1)}) %all-gather.10.cloned.1.call-update) | async-done | bytes 4194320 | tf_op jit(solution)/shard_map/all_gather | solution.py:593
  351.7 7.1 fusion.34.dprod_ref
  358.8 35.2 %mixer_backward.1 = (bf16[1024,640]{1,0:T(8,128)(2,1)}, bf16[1024,1280]{1,0:T(8,128)(2,1)}, bf16[1024,640]{1,0:T(8,128)(2,1)}, f32[8,8,640]{2,1,0:T(8,128)}) custom-call(f32[1024,640]{1,0:T(8,128)} %fusion.34.dprod_ref, f32[1024,640]{1,0:T(8,128)} %fusion.30.gated_ref, f32[1024,640]{1,0:T(8,128)} %get-tuple-element.31.states_ref, ...), custom_call_target="tpu_custom_call" | custom-call | flops 3355443200 | bytes 17039360 | tf_op jit(solution)/shard_map/mixer_backward/pallas_call | solution.py:246
  394.0 3.7 fusion.36
  400.3 5.7 fusion.35
  406.0 5.1 add_convert_fusion
  411.2 11.1 %convolution_convert_fusion = bf16[1024,2048]{1,0:T(8,128)(2,1)} fusion(bf16[1024,1536]{1,0:T(8,128)(2,1)} %get-tuple-element.100.refs_4_, bf16[1536,2048]{1,0:T(8,128)(2,1)} %param.34), kind=kOutput, calls=%fused_computation.14 | convolution fusion | flops 6444548096 | bytes 13631488 | tf_op jit(solution)/shard_map/dot_general | solution.py:572
  422.3 383.1 %dp_scatter.1 = (f32[256,1536]{1,0:T(8,128)}, f32[256,1536]{1,0:T(8,128)}, f32[256,1536]{1,0:T(8,128)}, f32[256,640]{1,0:T(8,128)}, f32[256,640]{1,0:T(8,128)}, ...) custom-call(bf16[1024,2048]{1,0:T(8,128)(2,1)} %bitcast.80, ...), custom_call_target="tpu_custom_call" | custom-call | flops 27380416512 | bytes 53477376 | tf_op jit(solution)/shard_map/dp_scatter/pallas_call | solution.py:544
  805.4 3.1 copy.44
  817.0 41.6 %psum.14 = f32[4096]{0:T(1024)S(1)} all-reduce(f32[4096]{0:T(1024)S(1)} %pad_maximum_fusion.3), channel_id=1, replica_groups=mesh['dp'=8,'tensor'=4] {'dp','tensor'}, use_global_device_ids=true, to_apply=%region_10.11 | all-reduce | flops 4096 | bytes 32768 | tf_op jit(solution)/shard_map/psum | solution.py:656
  859.3 5.7 fusion.6
  (143 shorter events, 26.8 us)
Async XLA Ops:
  7.2 81.6 %copy-start = (bf16[640,2048]{1,0:T(8,128)(2,1)S(1)}, bf16[640,2048]{1,0:T(8,128)(2,1)}, u32[]{:S(2)}) copy-start(bf16[640,2048]{1,0:T(8,128)(2,1)} %param.30) | copy-start | bytes 7864324
  7.2 5.5 copy-start.28
  7.2 6.5 copy-start.17
  7.2 6.5 copy-start.16
  7.2 42.7 %all-gather.6.cloned.1.call-start = ((), (), s32[]{:S(2)}) async-start(), calls=%async_computation.4 | async-start | bytes 5242880 | tf_op jit(solution)/shard_map/all_gather | solution.py:593
  12.6 127.2 %reduce-scatter.5.cloned.1.call-start = ((), (), s32[]{:S(2)}) async-start(), calls=%async_computation.5 | async-start | bytes 5242880 | tf_op jit(solution)/shard_map/reduce_scatter | solution.py:594
  16.6 5.0 copy-start.31
  16.6 5.0 copy-start.25
  49.9 8.1 copy-start.32
  49.9 8.1 copy-start.34
  95.1 46.8 %copy-start.19 = (f32[2048]{0:T(1024)S(1)}, f32[2048]{0:T(1024)}, u32[]{:S(2)}) copy-start(f32[2048]{0:T(1024)} %param.31) | copy-start | bytes 24580
  95.1 83.0 %all-gather.8.cloned.1.call-start = ((), (), s32[]{:S(2)}) async-start(), calls=%async_computation.6 | async-start | bytes 5242880 | tf_op jit(solution)/shard_map/all_gather | solution.py:593
  143.5 70.6 %all-gather.12.cloned.1.call-start = ((), (), s32[]{:S(2)}) async-start(), calls=%async_computation.12 | async-start | bytes 5242880 | tf_op jit(solution)/shard_map/all_gather | solution.py:593
  144.0 167.2 %reduce-scatter.9.cloned.1.call-start = ((), (), s32[]{:S(2)}) async-start(), calls=%async_computation.8 | async-start | bytes 5242880 | tf_op jit(solution)/shard_map/reduce_scatter | solution.py:594
  178.1 12.6 %copy-start.33 = (bf16[1024,2048]{1,0:T(8,128)(2,1)S(1)}, bf16[1024,2048]{1,0:T(8,128)(2,1)}, u32[]{:S(2)}) copy-start(bf16[1024,2048]{1,0:T(8,128)(2,1)} %all-gather.8.cloned.1.call-done.refs_1_) | copy-start | bytes 12582916
  231.5 11.1 %copy-start.37 = (bf16[1024,1536]{1,0:T(8,128)(2,1)}, bf16[1024,1536]{1,0:T(8,128)(2,1)S(1)}, u32[]{:S(2)}) copy-start(bf16[1024,1536]{1,0:T(8,128)(2,1)S(1)} %get-tuple-element.99.refs_5_) | copy-start | bytes 9437188
  231.5 11.1 %copy-start.38 = (bf16[1024,1536]{1,0:T(8,128)(2,1)}, bf16[1024,1536]{1,0:T(8,128)(2,1)S(1)}, u32[]{:S(2)}) copy-start(bf16[1024,1536]{1,0:T(8,128)(2,1)S(1)} %get-tuple-element.98.refs_6_) | copy-start | bytes 9437188
  266.6 85.1 %all-gather.10.cloned.1.call-start = ((), (), s32[]{:S(2)}) async-start(), calls=%async_computation.9 | async-start | bytes 5242880 | tf_op jit(solution)/shard_map/all_gather | solution.py:593
  317.1 492.5 %all-reduce.4.cloned.1.call-start = ((), (), s32[]{:S(2)}) async-start(), calls=%async_computation.11 | async-start | bytes 1679360 | tf_op jit(solution)/shard_map/psum | solution.py:652
  358.8 35.2 %copy-start.9 = (bf16[1024,640]{1,0:T(8,128)(2,1)S(1)}, bf16[1024,640]{1,0:T(8,128)(2,1)}, u32[]{:S(2)}) copy-start(bf16[1024,640]{1,0:T(8,128)(2,1)} %get-tuple-element.32.conv_ref) | copy-start | bytes 3932164
  400.2 414.9 %reduce-scatter.11.cloned.1.call-start = ((), (), s32[]{:S(2)}) async-start(), calls=%async_computation.10 | async-start | bytes 5242880 | tf_op jit(solution)/shard_map/reduce_scatter | solution.py:594
  400.2 5.8 copy-start.35
  400.2 5.8 copy-start.36
  411.1 448.2 %reduce-scatter.7.cloned.1.call-start = ((), (), s32[]{:S(2)}) async-start(), calls=%async_computation.7 | async-start | bytes 5242880 | tf_op jit(solution)/shard_map/reduce_scatter | solution.py:594
  808.5 5.2 copy-start.24
  808.5 6.6 copy-start.4
  808.5 6.6 copy-start.20
  808.5 6.6 copy-start.22
  809.6 49.1 %copy-start.27 = (f32[256]{0:T(256)S(1)}, f32[256]{0:T(256)}, u32[]{:S(2)}) copy-start(f32[256]{0:T(256)} %copy-done.26) | copy-start | bytes 3076
  810.8 48.5 %copy-start.7 = (bf16[256,2048]{1,0:T(8,128)(2,1)S(1)}, bf16[256,2048]{1,0:T(8,128)(2,1)}, u32[]{:S(2)}) copy-start(bf16[256,2048]{1,0:T(8,128)(2,1)} %reduce-scatter.5.cloned.1.call-done) | copy-start | bytes 3145732
  859.3 6.6 copy-start.12
  859.3 5.7 copy-start.13
  (17 other events, 47.0 us)
Sparse Core Ops, SparseCore 0:
  12.7 37.1 all-gather.5
  95.2 44.5 reduce-scatter.4
  143.6 34.4 all-gather.7
  179.6 34.4 all-gather.11
  266.7 44.5 reduce-scatter.8
  317.2 34.4 all-gather.9
  400.3 80.8 all-reduce.3
  483.7 46.4 reduce-scatter.10
  532.9 44.5 reduce-scatter.6

commit v2 on v1

v2 whole, which is shorter than its diff:
```python
import functools

import jax
import jax.numpy as jnp
from jax import lax
from jax.experimental import pallas as pl
from jax.experimental.pallas import tpu as pltpu
from jax.sharding import PartitionSpec as P

epsilon = 1e-06
decay_scale = 8.0
LANES = 128
GELU_C = 0.7978845608028654
GELU_K = 0.044715
F32 = jnp.float32
BF16 = jnp.bfloat16
VMEM_BYTES = 60 * 1024 * 1024


def minus_expm1(y, exp_y):
    s = 1.0 + y * (1.0 / 9.0)
    for d in range(8, 1, -1):
        s = 1.0 + (y * (1.0 / d)) * s
    return jnp.where(y > -0.5, -y * s, 1.0 - exp_y)


def gelu_parts(v):
    v2 = v * v
    t = jnp.tanh(GELU_C * v * (1.0 + GELU_K * v2))
    half = 0.5 * (1.0 + t)
    slope = half + 0.5 * v * (1.0 - t * t) * (GELU_C * (1.0 + 3.0 * GELU_K * v2))
    return v * half, slope


def lane_tiles(width):
    return [slice(j * LANES, (j + 1) * LANES) for j in range(width // LANES)]


def fold_rows(v):
    return jnp.sum(v.reshape(v.shape[0] // 8, 8, v.shape[1]), axis=0)


def gates_pre(rows, step, conv_ref, w_ref, pre_s):
    @pl.loop(0, rows // step)
    def _(i):
        r = pl.ds(pl.multiple_of(i * step, step), step)
        pre_s[r, :] = jnp.dot(conv_ref[r, :], w_ref[...], preferred_element_type=F32)


def mixer_forward_kernel(branch_ref, gated_ref, mask_ref, vec_ref, w_ref, conv_ref, states_ref, product_ref, pre_s, a_s, b_s):
    rows, width = branch_ref.shape
    seg = rows // 8
    tiles = lane_tiles(width)

    @pl.loop(0, 8)
    def _(s):
        t0 = pl.multiple_of(s * seg, seg)
        before = pl.multiple_of(jnp.maximum(t0 - 8, 0), 8)
        same = [mask_ref[pl.ds(t0, seg), k : k + 1] for k in range(3)]
        for cols in tiles:
            b = branch_ref[pl.ds(t0, seg), cols]
            ext = jnp.concatenate([branch_ref[pl.ds(before, 8), cols], b], axis=0)
            out = vec_ref[4:5, cols] + vec_ref[0:1, cols] * b
            for k in range(1, 4):
                out = out + vec_ref[k : k + 1, cols] * pltpu.roll(ext, k, 0)[8:] * same[k - 1]
            conv_ref[pl.ds(t0, seg), cols] = out.astype(BF16)

    gates_pre(rows, 256, conv_ref, w_ref, pre_s)

    @pl.loop(0, 8)
    def _(s):
        t0 = pl.multiple_of(s * seg, seg)
        c = mask_ref[pl.ds(t0, seg), 0:1]
        for j, cols in enumerate(tiles):
            cols_i = slice(width + j * LANES, width + (j + 1) * LANES)
            r = jax.nn.sigmoid(pre_s[pl.ds(t0, seg), cols] + vec_ref[5:6, cols])
            i = jax.nn.sigmoid(pre_s[pl.ds(t0, seg), cols_i] + vec_ref[6:7, cols])
            log_a = (-decay_scale * vec_ref[7:8, cols]) * r
            a = jnp.exp(log_a)
            n = jnp.sqrt(minus_expm1(2.0 * log_a, a * a))
            mult = (1.0 - c) + c * n
            a_s[j, pl.ds(t0, seg), :] = a * c
            b_s[j, pl.ds(t0, seg), :] = mult * i * conv_ref[pl.ds(t0, seg), cols].astype(F32)

    def scan_step(i, carry):
        out = []
        for j in range(len(tiles)):
            h, p = carry[j]
            at = pl.ds(i, 8, stride=seg)
            a = a_s[j, at, :]
            h = a * h + b_s[j, at, :]
            p = a * p
            b_s[j, at, :] = h
            a_s[j, at, :] = p
            out.append((h, p))
        return tuple(out)

    one = jnp.ones((8, LANES), F32)
    lax.fori_loop(0, seg, scan_step, tuple((jnp.zeros((8, LANES), F32), one) for _ in tiles), unroll=4)

    def finish(s, carry):
        t0 = pl.multiple_of(s * seg, seg)
        out = []
        for j, cols in enumerate(tiles):
            st = b_s[j, pl.ds(t0, seg), :] + a_s[j, pl.ds(t0, seg), :] * carry[j]
            states_ref[pl.ds(t0, seg), cols] = st
            act, _ = gelu_parts(gated_ref[pl.ds(t0, seg), cols])
            product_ref[pl.ds(t0, seg), cols] = (st * act).astype(BF16)
            out.append(st[seg - 1 : seg, :])
        return tuple(out)

    lax.fori_loop(0, 8, finish, tuple(jnp.zeros((1, LANES), F32) for _ in tiles))


class MixerBackward:
    def __init__(self, masks, vecs, w_cat, states, branch, conv, dgated, dri, dbranch, sums, pre_s, a_s, n_s, ac_s, e_s, p_s):
        self.masks, self.vecs, self.w_cat, self.states, self.branch, self.conv = masks, vecs, w_cat, states, branch, conv
        self.dgated, self.dri, self.dbranch, self.sums = dgated, dri, dbranch, sums
        self.pre_s, self.a_s, self.n_s, self.ac_s, self.e_s, self.p_s = pre_s, a_s, n_s, ac_s, e_s, p_s
        self.rows, self.width = states.shape
        self.seg = self.rows // 8
        self.tiles = lane_tiles(self.width)

    @staticmethod
    def scratch(rows, width):
        lanes = width // LANES
        return [
            pltpu.VMEM((rows, 2 * width), F32),
            pltpu.VMEM((rows, width), F32),
            pltpu.VMEM((rows + 8, width), F32),
            pltpu.VMEM((lanes, rows + 8, LANES), F32),
            pltpu.VMEM((lanes, rows, LANES), F32),
            pltpu.VMEM((lanes, rows, LANES), F32),
        ]

    def gates(self):
        self.sums[...] = jnp.zeros_like(self.sums)
        gates_pre(self.rows, 256, self.conv, self.w_cat, self.pre_s)

    def factors(self, gated):
        @pl.loop(0, 8)
        def _(s):
            t0 = pl.multiple_of(s * self.seg, self.seg)
            at = pl.ds(t0, self.seg)
            c = self.masks[at, 0:1]
            for j, cols in enumerate(self.tiles):
                cols_i = slice(self.width + j * LANES, self.width + (j + 1) * LANES)
                r = jax.nn.sigmoid(self.pre_s[at, cols] + self.vecs[5:6, cols])
                self.pre_s[at, cols] = r
                self.pre_s[at, cols_i] = jax.nn.sigmoid(self.pre_s[at, cols_i] + self.vecs[6:7, cols])
                log_a = (-decay_scale * self.vecs[7:8, cols]) * r
                a = jnp.exp(log_a)
                d = self.a_s[at, cols]
                self.a_s[at, cols] = a
                self.n_s[at, cols] = jnp.sqrt(minus_expm1(2.0 * log_a, a * a))
                self.ac_s[j, at, :] = a * c
                act, slope = gelu_parts(gated[at, cols])
                self.e_s[j, at, :] = d * act
                self.dgated[at, cols] = (d * self.states[at, cols] * slope).astype(BF16)

    def scan(self):
        seg, lanes = self.seg, len(self.tiles)
        for j in range(lanes):
            self.ac_s[j, self.rows : self.rows + 8, :] = jnp.zeros((8, LANES), F32)

        def step(q, carry):
            i = seg - 1 - q
            out = []
            for j in range(lanes):
                e, p = carry[j]
                at = pl.ds(i, 8, stride=seg)
                a = self.ac_s[j, pl.ds(i + 1, 8, stride=seg), :]
                e = a * e + self.e_s[j, at, :]
                p = a * p
                self.e_s[j, at, :] = e
                self.p_s[j, at, :] = p
                out.append((e, p))
            return tuple(out)

        one = jnp.ones((8, LANES), F32)
        lax.fori_loop(0, seg, step, tuple((jnp.zeros((8, LANES), F32), one) for _ in self.tiles), unroll=4)

    def gate_gradients(self):
        seg, width = self.seg, self.width

        def finish(q, carry):
            s = 7 - q
            t0 = pl.multiple_of(s * seg, seg)
            at = pl.ds(t0, seg)
            before = pl.multiple_of(jnp.maximum(t0 - 8, 0), 8)
            c = self.masks[at, 0:1]
            out = []
            for j, cols in enumerate(self.tiles):
                cols_i = slice(width + j * LANES, width + (j + 1) * LANES)
                e = self.e_s[j, at, :] + self.p_s[j, at, :] * carry[j]
                out.append(e[0:1, :])
                ext = jnp.concatenate([self.states[pl.ds(before, 8), cols], self.states[at, cols]], axis=0)
                earlier = pltpu.roll(ext, 1, 0)[8:]
                r, i, a, n = self.pre_s[at, cols], self.pre_s[at, cols_i], self.a_s[at, cols], self.n_s[at, cols]
                cv = self.conv[at, cols].astype(F32)
                ec = e * c
                d_log = a * (ec * earlier) - ec * i * cv * (a * a / n)
                rr = d_log * r
                dr = ((-decay_scale * self.vecs[7:8, cols]) * rr * (1.0 - r)).astype(BF16)
                em = e * ((1.0 - c) + c * n) * i
                di = (em * cv * (1.0 - i)).astype(BF16)
                self.dri[at, cols] = dr
                self.dri[at, cols_i] = di
                self.n_s[at, cols] = em
                self.sums[5, :, cols] += fold_rows(dr.astype(F32))
                self.sums[6, :, cols] += fold_rows(di.astype(F32))
                self.sums[7, :, cols] += fold_rows(rr)
            return tuple(out)

        lax.fori_loop(0, 8, finish, tuple(jnp.zeros((1, LANES), F32) for _ in self.tiles))

        @pl.loop(0, self.rows // 256)
        def _(i):
            at = pl.ds(pl.multiple_of(i * 256, 256), 256)
            self.n_s[at, :] += dot_nt(self.dri[at, :], self.w_cat[...])

        self.n_s[self.rows : self.rows + 8, :] = jnp.zeros((8, width), F32)

    def convolution(self):
        @pl.loop(0, 8)
        def _(s):
            t0 = pl.multiple_of(s * self.seg, self.seg)
            at, ext = pl.ds(t0, self.seg), pl.ds(t0, self.seg + 8)
            same = [self.masks[ext, k : k + 1] for k in range(3)]
            for cols in self.tiles:
                d = self.n_s[ext, cols]
                b = self.branch[at, cols]
                self.sums[4, :, cols] += fold_rows(d[: self.seg])
                self.sums[0, :, cols] += fold_rows(d[: self.seg] * b)
                total = self.vecs[0:1, cols] * d[: self.seg]
                for k in range(1, 4):
                    moved = pltpu.roll(d * same[k - 1], self.seg + 8 - k, 0)[: self.seg]
                    total = total + self.vecs[k : k + 1, cols] * moved
                    self.sums[k, :, cols] += fold_rows(moved * b)
                self.dbranch[at, cols] = total.astype(BF16)


def dot_nt(left, right):
    return lax.dot_general(left, right, (((1,), (1,)), ((), ())), preferred_element_type=F32)


class Stage:
    def __init__(self, stride, size, later):
        self.stride, self.size, self.later = stride, size, later
        self.blocks = 1
        for s in later:
            self.blocks *= s.size
        self.digit = lax.rem(lax.axis_index("dp") // stride, size)

    def offset(self, position):
        total = 0
        for s in reversed(self.later):
            total = total + lax.rem(position, s.size) * s.stride
            position = position // s.size
        return total


def digit_sizes(n):
    if n == 8:
        return [2, 4]
    sizes = []
    while n > 1:
        m = 4 if n % 4 == 0 else 2 if n % 2 == 0 else n
        sizes.append(m)
        n //= m
    return sizes


def make_stages(n, last_first):
    digits, stride = [], 1
    for m in digit_sizes(n):
        digits.append((stride, m))
        stride *= m
    if last_first:
        digits = digits[1:] + digits[:1]
    stages = []
    for stride, m in reversed(digits):
        stages.insert(0, Stage(stride, m, list(stages)))
    return stages


class Item:
    def __init__(self, stages, left, right, width, ready, refs):
        self.stages, self.left, self.right, self.width, self.ready = stages, left, right, width, ready
        self.columns = right.shape[1]
        self.out, self.recv, self.send, self.send_sem, self.recv_sem = refs

    def message(self, t, back, k, slot, rows=None):
        stage = self.stages[t]
        rows = pl.ds(0, stage.blocks * self.width) if rows is None else rows
        step = jnp.where(back, -stage.stride, stage.stride)
        return pltpu.make_async_remote_copy(
            src_ref=self.send[t].at[slot, rows],
            dst_ref=self.recv[t].at[back, k - 1, rows],
            send_sem=self.send_sem[t].at[slot],
            recv_sem=self.recv_sem[t].at[back, k - 1],
            device_id={"dp": lax.axis_index("dp") + step},
            device_id_type=pl.DeviceIdType.MESH,
        )


class Engine:
    def __init__(self, left_s, got_s, total_s, sem):
        self.left_s, self.got_s, self.total_s, self.sem = left_s, got_s, total_s, sem

    def product(self, item, block, store):
        if len(item.left.shape) == 3:
            source = item.left.at[block]
        else:
            source = item.left.at[:, pl.ds(pl.multiple_of(block * item.width, item.width), item.width)]
        fetch = pltpu.make_async_copy(source, self.left_s, self.sem.at[0])
        fetch.start()
        fetch.wait()
        tile = 512 if item.columns % 512 == 0 else item.columns
        for c in range(item.columns // tile):
            cols = pl.ds(c * tile, tile)
            store(cols, lax.dot_general(self.left_s[...], item.right[:, cols], (((0,), (0,)), ((), ())), preferred_element_type=F32))

    def add_gots(self, item, rows, gots, store):
        copies = []
        for i, (condition, source) in enumerate(gots):
            copy = pltpu.make_async_copy(source, self.got_s.at[i, :, pl.ds(0, item.columns)], self.sem.at[1 + i])
            copies.append(copy)

            @pl.when(condition)
            def _(copy=copy):
                copy.start()

        for (condition, _), copy in zip(gots, copies):

            @pl.when(condition)
            def _(copy=copy):
                copy.wait()

        @pl.loop(0, item.width // 16)
        def _(r):
            at = pl.ds(pl.multiple_of(r * 16, 16), 16)
            here = pl.ds(pl.multiple_of(rows + r * 16, 16), 16)
            total = self.total_s[here, pl.ds(0, item.columns)]
            for i, (condition, _) in enumerate(gots):
                total = total + jnp.where(condition, self.got_s[i, at, pl.ds(0, item.columns)].astype(F32), 0.0)
            store(here, total)

    def arrived(self, item, t, position):
        found = []
        for u in range(t):
            stage = item.stages[u]
            spot = position
            rows = None
            scale = 1
            for s in item.stages[t:]:
                scale *= s.size
            lead = 0
            for s in item.stages[u + 1 : t]:
                lead = lead * s.size + s.digit
            rows = pl.ds((lead * scale + spot) * item.width, item.width)
            last = stage.size - 2
            if stage.size == 2:
                back = jnp.where(stage.digit == 0, 1, 0)
                found.append((stage.digit >= 0, item.recv[u].at[back, last, rows]))
            else:
                found.append((stage.digit >= 1, item.recv[u].at[0, last, rows]))
                found.append((stage.digit <= stage.size - 2, item.recv[u].at[1, last, rows]))
        return found

    def own_base(self, item, t):
        base = 0
        for s in item.stages[:t]:
            base = base + s.digit * s.stride
        return base

    def wait_last(self, item, t):
        if t < item.ready:
            return
        stage = item.stages[t]
        for back in range(2):
            me = stage.digit if back == 0 else stage.size - 1 - stage.digit

            @pl.when(me >= 1)
            def _(back=back):
                item.message(t, back, stage.size - 1, 0).wait_recv()

    def round(self, item, t, k):
        stage = item.stages[t]
        base = self.own_base(item, t)
        alone = t == 0 and k == 1

        @pl.loop(0, 2)
        def _(back):
            me = jnp.where(back == 0, stage.digit, stage.size - 1 - stage.digit)
            there = me + stage.size - k
            value = jnp.where(back == 0, there, stage.size - 1 - there)
            slot = jnp.where(value > stage.digit, value - 1, value)

            @pl.when(me <= k - 1)
            def _():
                @pl.loop(0, stage.blocks)
                def _(p):
                    at = pl.ds(pl.multiple_of(p * item.width, item.width), item.width)

                    def store(cols, total):
                        if alone:
                            item.send[t][slot, at, cols] = total.astype(BF16)
                        else:
                            self.total_s[at, cols] = total

                    self.product(item, base + value * stage.stride + stage.offset(p), store)
                    if alone:
                        item.message(t, back, k, slot, at).start()

            if k == 1 and t > 0:

                @pl.when(back == 0)
                def _():
                    self.wait_last(item, t - 1)

            if not alone:

                @pl.when(me <= k - 1)
                def _():
                    if k > 1:

                        @pl.when(me >= 1)
                        def _():
                            item.message(t, back, k - 1, 0).wait_recv()

                    @pl.loop(0, stage.blocks)
                    def _(p):
                        rows = pl.multiple_of(p * item.width, item.width)
                        at = pl.ds(rows, item.width)
                        gots = self.arrived(item, t, value * stage.blocks + p)
                        if k > 1:
                            gots.append((me >= 1, item.recv[t].at[back, k - 2, at]))

                        def store(here, total):
                            item.send[t][slot, here, :] = total.astype(BF16)

                        self.add_gots(item, rows, gots, store)
                        item.message(t, back, k, slot, at).start()

    def finish(self, item):
        t = len(item.stages)

        def store(cols, total):
            self.total_s[pl.ds(0, item.width), cols] = total

        self.product(item, self.own_base(item, t), store)
        self.wait_last(item, t - 1)

        def store_sum(here, total):
            self.total_s[here, pl.ds(0, item.columns)] = total

        self.add_gots(item, 0, self.arrived(item, t, 0), store_sum)
        copy = pltpu.make_async_copy(self.total_s.at[pl.ds(0, item.width), pl.ds(0, item.columns)], item.out, self.sem.at[0])
        copy.start()
        copy.wait()

    def drain(self, item, stages):
        for t in stages:
            for slot in range(item.stages[t].size - 1):
                item.message(t, 0, 1, slot).wait_send()


def stage_shapes(n, last_first, width, columns):
    sizes = digit_sizes(n)
    if last_first:
        sizes = sizes[1:] + sizes[:1]
    left, found = n, []
    for t, m in enumerate(sizes):
        left //= m
        found.append(
            (
                jax.ShapeDtypeStruct((2, m - 1, left * width, columns), BF16),
                pltpu.VMEM((m - 1, left * width, columns), BF16),
                pltpu.SemaphoreType.DMA((m - 1,)),
                pltpu.SemaphoreType.DMA((2, m - 1)),
                left * width if t > 0 or m > 2 else width,
            )
        )
    return found


class Reader:
    def __init__(self, refs):
        self.refs, self.at = refs, 0

    def __call__(self, count=None):
        start = self.at
        self.at += 1 if count is None else count
        return self.refs[start] if count is None else list(self.refs[start : self.at])


def column_blocks(left, n):
    tokens, features = left.shape
    width = features // n
    return left.reshape(tokens, n, width).transpose(1, 0, 2) if width % LANES else left


class TensorLine:
    def __init__(self):
        self.index = lax.axis_index("tensor")
        self.mate, self.peer, self.cross = self.index ^ 1, self.index ^ 2, self.index ^ 3


def copy_in(source, target, sem):
    copy = pltpu.make_async_copy(source, target, sem)
    copy.start()
    return copy


def remote(source, target, send_sem, recv_sem, axis, index):
    return pltpu.make_async_remote_copy(
        src_ref=source, dst_ref=target, send_sem=send_sem, recv_sem=recv_sem,
        device_id={axis: index}, device_id_type=pl.DeviceIdType.MESH,
    )


class TensorReduce:
    def __init__(self, line, part, from_mate, from_peer, own_v, got_v, send_v, send_sem, recv_sem, sem):
        self.line, self.part, self.from_mate, self.from_peer = line, part, from_mate, from_peer
        self.own_v, self.got_v, self.send_v, self.sem = own_v, got_v, send_v, sem
        self.rows = part.shape[0] // 4
        self.mates = [
            remote(self.block(line.cross), from_mate.at[0], send_sem.at[0], recv_sem.at[0], "tensor", line.mate),
            remote(self.block(line.mate), from_mate.at[1], send_sem.at[1], recv_sem.at[1], "tensor", line.mate),
        ]
        self.over = remote(send_v, from_peer, send_sem.at[2], recv_sem.at[2], "tensor", line.peer)

    def block(self, index):
        return self.part.at[pl.ds(pl.multiple_of(index * self.rows, self.rows), self.rows)]

    def start(self):
        for copy in self.mates:
            copy.start()

    def middle(self):
        own = copy_in(self.block(self.line.peer), self.own_v, self.sem.at[0])
        self.mates[0].wait_recv()
        got = copy_in(self.from_mate.at[0], self.got_v.at[0], self.sem.at[1])
        own.wait()
        got.wait()

        @pl.loop(0, self.rows // 16)
        def _(r):
            at = pl.ds(pl.multiple_of(r * 16, 16), 16)
            self.send_v[at, :] = (self.own_v[at, :].astype(F32) + self.got_v[0, at, :].astype(F32)).astype(BF16)

        self.over.start()

    def end(self, use):
        own = copy_in(self.block(self.line.index), self.own_v, self.sem.at[0])
        self.mates[1].wait_recv()
        got = copy_in(self.from_mate.at[1], self.got_v.at[0], self.sem.at[1])
        self.over.wait_recv()
        over = copy_in(self.from_peer, self.got_v.at[1], self.sem.at[2])
        own.wait()
        got.wait()
        over.wait()

        @pl.loop(0, self.rows // 16)
        def _(r):
            at = pl.ds(pl.multiple_of(r * 16, 16), 16)
            use(at, self.own_v[at, :].astype(F32) + self.got_v[0, at, :].astype(F32) + self.got_v[1, at, :].astype(F32))

    def drain(self):
        for copy in self.mates:
            copy.wait_send()
        self.over.wait_send()

    @staticmethod
    def results(tokens, features):
        return [jax.ShapeDtypeStruct((2, tokens // 4, features), BF16), jax.ShapeDtypeStruct((tokens // 4, features), BF16)]

    @staticmethod
    def semaphores():
        return [pltpu.SemaphoreType.DMA((3,)), pltpu.SemaphoreType.DMA((3,)), pltpu.SemaphoreType.DMA((3,))]

    @staticmethod
    def buffers(tokens, features):
        rows = tokens // 4
        return [pltpu.VMEM((rows, features), BF16), pltpu.VMEM((2, rows, features), BF16), pltpu.VMEM((rows, features), BF16)]


def norm_backward(values, gain, d_normed):
    inverse = lax.rsqrt(jnp.mean(values * values, axis=-1, keepdims=True) + epsilon)
    weighted = gain * d_normed
    inner = jnp.mean(weighted * values, axis=-1, keepdims=True)
    return inverse * weighted - values * (inverse * inverse * inverse * inner), d_normed * values * inverse


HBM = pl.BlockSpec(memory_space=pl.ANY)
IN_VMEM = pl.BlockSpec(memory_space=pltpu.VMEM)


def chain_kernel(n, width, *refs):
    take = Reader(refs)
    part, middle, cot_own, w_out, gated, branch, states, conv = take(8)
    gain, masks, vecs, w_cat = take(4)
    left_down, left_gate, right_down, right_gate = take(4)
    d_middle, att, dgated_o, dri_o, dbranch_o, from_mate, from_peer, down_recv, gate_recv = take(9)
    sums, gain_grad = take(2)
    down_v, down_send, down_ss, down_rs, gate_send, gate_ss, gate_rs = take(7)
    left_s, got_s, total_s, rs_send, rs_recv, rs_sem, ag_send, ag_recv, sem, engine_sem = take(10)
    tokens, features = part.shape
    rows, channels = tokens // 4, conv.shape[1]
    line = TensorLine()
    engine = Engine(left_s, got_s, total_s, engine_sem)
    down_load = copy_in(right_down, down_v, sem.at[6])
    down = Item(make_stages(n, True), left_down, down_v, width, 0, (None, [down_recv], [down_send], [down_ss], [down_rs]))

    def rounds(item):
        return list(range(1, item.stages[0].size))

    def att_rows(index):
        return att.at[pl.ds(pl.multiple_of(index * rows, rows), rows)]

    first, between, last = rounds(down)[:1], rounds(down)[1:-1], rounds(down)[1:][-1:]

    def tensor_phase(gate_v, own_v, got_v, send_v, middle_v, cot_v, dmid_v, att_v):
        reduce = TensorReduce(line, part, from_mate, from_peer, own_v, got_v, send_v, rs_send, rs_recv, rs_sem)
        reduce.start()
        gate_load = copy_in(right_gate, gate_v, sem.at[7])
        loads = [copy_in(middle, middle_v, sem.at[0]), copy_in(cot_own, cot_v, sem.at[1])]
        gate = Item(make_stages(n, False), left_gate, gate_v, width, 0, (None, [gate_recv], [gate_send], [gate_ss], [gate_rs]))
        down_load.wait()
        for k in first:
            engine.round(down, 0, k)
        reduce.middle()
        gate_load.wait()
        for k in rounds(gate):
            engine.round(gate, 0, k)
        for load in loads:
            load.wait()
        gain_grad[...] = jnp.zeros_like(gain_grad)

        def use(at, total):
            back, terms = norm_backward(middle_v[at, :], gain[...], total)
            value = cot_v[at, :].astype(F32) + back
            dmid_v[at, :] = value
            att_v[at, :] = value.astype(BF16)
            gain_grad[...] += fold_rows(terms)

        reduce.end(use)
        across = [
            remote(att_v, att_rows(line.index), ag_send.at[0], ag_recv.at[0], "tensor", line.peer),
            remote(att_v, att_rows(line.index), ag_send.at[1], ag_recv.at[1], "tensor", line.mate),
        ]
        for copy in across:
            copy.start()
        keep = [copy_in(att_v, att_rows(line.index), sem.at[0]), copy_in(dmid_v, d_middle, sem.at[1])]
        for k in between:
            engine.round(down, 0, k)
        across[0].wait_recv()
        forward = remote(att_rows(line.peer), att_rows(line.peer), ag_send.at[2], ag_recv.at[2], "tensor", line.mate)
        forward.start()
        across[1].wait_recv()
        forward.wait_recv()
        for copy in keep:
            copy.wait()
        for copy in [*across, forward]:
            copy.wait_send()
        reduce.drain()
        for t in (0,):
            engine.drain(gate, [t])
            engine.wait_last(gate, t)

    pl.run_scoped(
        tensor_phase,
        pltpu.VMEM(right_gate.shape, BF16),
        *TensorReduce.buffers(tokens, features),
        pltpu.VMEM((rows, features), F32),
        pltpu.VMEM((rows, features), BF16),
        pltpu.VMEM((rows, features), F32),
        pltpu.VMEM((rows, features), BF16),
    )

    def mixer_phase(gated_v, states_v, conv_v, dgated_v, dri_v, dbranch_v, att_v, w_v, *scratch):
        w_load = copy_in(w_out, w_v, sem.at[0])
        blocks = [copy_in(att_rows(0), att_v.at[0], sem.at[4])]
        loads = [copy_in(conv, conv_v, sem.at[1]), copy_in(gated, gated_v, sem.at[2]), copy_in(states, states_v, sem.at[3])]
        mixer = MixerBackward(masks, vecs, w_cat, states_v, gated_v, conv_v, dgated_v, dri_v, dbranch_v, sums, *scratch)
        w_load.wait()
        for b in range(4):
            blocks[b].wait()
            if b < 3:
                blocks.append(copy_in(att_rows(b + 1), att_v.at[(b + 1) % 2], sem.at[4 + (b + 1) % 2]))
            mixer.a_s[pl.ds(b * rows, rows), :] = dot_nt(att_v[b % 2], w_v[...])
        loads[0].wait()
        mixer.gates()
        loads[1].wait()
        loads[2].wait()
        mixer.factors(gated_v)
        again = copy_in(branch, gated_v, sem.at[2])
        outs = [copy_in(dgated_v, dgated_o, sem.at[1])]
        for k in last:
            engine.round(down, 0, k)
        mixer.scan()
        mixer.gate_gradients()
        outs.append(copy_in(dri_v, dri_o, sem.at[3]))
        again.wait()
        mixer.convolution()
        outs.append(copy_in(dbranch_v, dbranch_o, sem.at[0]))
        for copy in outs:
            copy.wait()

    pl.run_scoped(
        mixer_phase,
        pltpu.VMEM((tokens, channels), F32),
        pltpu.VMEM((tokens, channels), F32),
        pltpu.VMEM((tokens, channels), BF16),
        pltpu.VMEM((tokens, channels), BF16),
        pltpu.VMEM((tokens, 2 * channels), BF16),
        pltpu.VMEM((tokens, channels), BF16),
        pltpu.VMEM((2, rows, features), BF16),
        pltpu.VMEM((channels, features), BF16),
        *MixerBackward.scratch(tokens, channels),
    )
    engine.drain(down, [0])
    engine.wait_last(down, 0)


def chain(part, middle, cot_own, w_out, gated_pre, branch_pre, states, conv_out, gain, masks, vecs, w_cat, cot, normed_two, hidden, d_gate):
    n = lax.axis_size("dp")
    tokens, features = part.shape
    channels, width = conv_out.shape[1], features // n
    down = stage_shapes(n, True, width, hidden.shape[1])[0]
    gate = stage_shapes(n, False, width, d_gate.shape[1])[0]
    tall = max(down[4], gate[4])
    dma = pltpu.SemaphoreType.DMA
    return pl.pallas_call(
        functools.partial(chain_kernel, n, width),
        out_shape=[
            jax.ShapeDtypeStruct((tokens // 4, features), F32),
            jax.ShapeDtypeStruct((tokens, features), BF16),
            jax.ShapeDtypeStruct((tokens, channels), BF16),
            jax.ShapeDtypeStruct((tokens, 2 * channels), BF16),
            jax.ShapeDtypeStruct((tokens, channels), BF16),
            *TensorReduce.results(tokens, features),
            down[0],
            gate[0],
            jax.ShapeDtypeStruct((8, 8, channels), F32),
            jax.ShapeDtypeStruct((8, features), F32),
        ],
        in_specs=[HBM] * 8 + [IN_VMEM] * 4 + [HBM] * 4,
        out_specs=[HBM] * 9 + [IN_VMEM] * 2,
        scratch_shapes=[
            pltpu.VMEM(hidden.shape, BF16), down[1], down[2], down[3], gate[1], gate[2], gate[3],
            pltpu.VMEM((tokens, width), BF16),
            pltpu.VMEM((1, width, hidden.shape[1]), BF16),
            pltpu.VMEM((tall, hidden.shape[1]), F32),
            *TensorReduce.semaphores(),
            dma((3,)), dma((3,)), dma((8,)), dma((2,)),
        ],
        compiler_params=pltpu.CompilerParams(vmem_limit_bytes=VMEM_BYTES, has_side_effects=True),
        cost_estimate=pl.CostEstimate(flops=12 * 10**9, bytes_accessed=60 * 10**6, transcendentals=8 * tokens * channels),
        name="chain",
    )(
        part, middle, cot_own, w_out, gated_pre, branch_pre, states, conv_out, gain, masks, vecs, w_cat,
        column_blocks(cot, n), column_blocks(normed_two, n), hidden, d_gate,
    )


def gather_sums(gains, sends, recvs, send_sems, recv_sems):
    n, line = lax.axis_size("dp"), TensorLine()
    hops = [("tensor", line.mate), ("tensor", line.peer)]
    bit = 1
    while bit < n:
        hops.append(("dp", lax.axis_index("dp") ^ bit))
        bit *= 2
    copies = [remote(sends.at[s], recvs.at[s], send_sems.at[s], recv_sems.at[s], *hop) for s, hop in enumerate(hops)]

    def begin(s):
        sends[s] = gains[...] if s == 0 else sends[s - 1] + recvs[s - 1]
        copies[s].start()

    def step(s):
        if s > 0:
            copies[s - 1].wait_recv()
        if s < len(copies):
            begin(s)
        else:
            gains[...] = sends[s - 1] + recvs[s - 1]
            for copy in copies:
                copy.wait_send()

    return [functools.partial(step, s) for s in range(len(copies) + 1)]


def finish_kernel(n, width, plan, order, lefts_of, readies, columns, *refs):
    take = Reader(refs)
    count = len(plan)
    part, part_out, middle, d_middle, stream = take(5)
    gain, gain_grad_two = take(2)
    lefts, rights_hbm = take(max(lefts_of) + 1), take(count)
    shapes = [stage_shapes(n, plan[i], width, columns[i]) for i in range(count)]
    given = [take(readies[i]) for i in range(count)]
    stream_grad_o, stream_out_o = take(2)
    outs = take(count)
    reduces = [take(2), take(2)]
    recv = [given[i] + take(len(shapes[i]) - readies[i]) for i in range(count)]
    (gains,) = take(1)
    rights = take(count)
    nones = [[None] * r for r in readies]
    sends = [nones[i] + take(len(shapes[i]) - readies[i]) for i in range(count)]
    send_sems = [nones[i] + take(len(shapes[i]) - readies[i]) for i in range(count)]
    recv_sems = [nones[i] + take(len(shapes[i]) - readies[i]) for i in range(count)]
    left_s, got_s, total_s, own_v, got_v, send_v, send_w = take(7)
    value_v, base_v, gain_sends, gain_recvs = take(4)
    rs_sems = [take(3), take(3)]
    gain_ss, gain_rs, right_sem, sem, engine_sem = take(5)

    line = TensorLine()
    engine = Engine(left_s, got_s, total_s, engine_sem)
    tensor = [
        TensorReduce(line, source, *reduces[q], own_v, got_v, (send_v, send_w)[q], *rs_sems[q])
        for q, source in enumerate((part, part_out))
    ]
    for reduce in tensor:
        reduce.start()
    loads = [copy_in(rights_hbm[i], rights[i], right_sem.at[i]) for i in range(count)]
    items = [
        Item(make_stages(n, plan[i]), lefts[lefts_of[i]], rights[i], width, readies[i], (outs[i], recv[i], sends[i], send_sems[i], recv_sems[i]))
        for i in range(count)
    ]

    def grad_end():
        copies = [copy_in(stream, value_v, sem.at[0]), copy_in(d_middle, base_v, sem.at[1])]
        for copy in copies:
            copy.wait()
        gains[...] = jnp.zeros_like(gains)

        def use(at, total):
            back, terms = norm_backward(value_v[at, :].astype(F32), gain[...], total)
            base_v[at, :] = base_v[at, :] + back
            gains[...] += fold_rows(terms)

        tensor[0].end(use)
        copy_in(base_v, stream_grad_o, sem.at[0]).wait()
        first = jnp.sum(gains[...], axis=0, keepdims=True)
        second = jnp.sum(gain_grad_two[...], axis=0, keepdims=True)
        pick = lax.broadcasted_iota(jnp.int32, gains.shape, 0)
        gains[...] = jnp.where(pick == 0, first, jnp.where(pick == 1, second, 0.0))

    def out_end():
        copy_in(middle, base_v, sem.at[0]).wait()

        def use(at, total):
            base_v[at, :] = base_v[at, :] + total

        tensor[1].end(use)
        copy_in(base_v, stream_out_o, sem.at[0]).wait()

    extra = [tensor[0].middle, tensor[1].middle, grad_end, out_end]
    extra += gather_sums(gains, gain_sends, gain_recvs, gain_ss, gain_rs)
    loaded = set()
    for i, t, k in order:
        if i < 0:
            if extra:
                extra.pop(0)()
            continue
        if i not in loaded:
            loads[i].wait()
            loaded.add(i)
        if t < len(shapes[i]):
            engine.round(items[i], t, k)
        else:
            engine.finish(items[i])
    for step in extra:
        step()
    for i, item in enumerate(items):
        engine.drain(item, range(readies[i], len(shapes[i])))
    for reduce in tensor:
        reduce.drain()


def task_order(plan, readies, names, n):
    tasks = []
    for last_first, ready in zip(plan, readies):
        sizes = digit_sizes(n)
        if last_first:
            sizes = sizes[1:] + sizes[:1]
        i = len(tasks)
        tasks.append([(i, t, k) for t, m in enumerate(sizes) for k in range(1, m) if t >= ready] + [(i, len(sizes), 0)])
    out, at = [], [0] * len(plan)
    for i in names:
        if i < 0:
            out.append((-1, 0, 0))
        elif at[i] < len(tasks[i]):
            out.append(tasks[i][at[i]])
            at[i] += 1
    for i in range(len(plan)):
        out += tasks[i][at[i] :]
    return out


def finish(part, part_out, middle, d_middle, stream, gain, gain_grad_two, lefts, lefts_of, rights, given, plan, names):
    n = lax.axis_size("dp")
    tokens, features = part.shape
    width, rows = features // n, tokens // 4
    readies = [len(g) for g in given]
    columns = [r.shape[1] for r in rights]
    widest = max(columns)
    shapes = [stage_shapes(n, last_first, width, c)[ready:] for last_first, c, ready in zip(plan, columns, readies)]
    steps = 2 + (n - 1).bit_length()
    dma = pltpu.SemaphoreType.DMA
    stream_shape = jax.ShapeDtypeStruct((rows, features), F32)
    out_shape = [stream_shape, stream_shape] + [jax.ShapeDtypeStruct((width, c), F32) for c in columns]
    out_shape += TensorReduce.results(tokens, features) * 2 + [s[0] for item in shapes for s in item]
    results = pl.pallas_call(
        functools.partial(finish_kernel, n, width, plan, task_order(plan, readies, names, n), lefts_of, readies, columns),
        out_shape=[*out_shape, jax.ShapeDtypeStruct((8, features), F32)],
        in_specs=[HBM] * 5 + [IN_VMEM] * 2 + [HBM] * (len(lefts) + len(rights) + sum(readies)),
        out_specs=[HBM] * len(out_shape) + [IN_VMEM],
        scratch_shapes=[
            *[pltpu.VMEM(r.shape, BF16) for r in rights],
            *[s[1] for item in shapes for s in item],
            *[s[2] for item in shapes for s in item],
            *[s[3] for item in shapes for s in item],
            pltpu.VMEM((tokens, width), BF16),
            pltpu.VMEM((2 * len(digit_sizes(n)), width, widest), BF16),
            pltpu.VMEM((max(s[4] for item in shapes for s in item), widest), F32),
            *TensorReduce.buffers(tokens, features),
            pltpu.VMEM((rows, features), BF16),
            pltpu.VMEM((rows, features), BF16),
            pltpu.VMEM((rows, features), F32),
            pltpu.VMEM((steps, 8, features), F32),
            pltpu.VMEM((steps, 8, features), F32),
            *TensorReduce.semaphores(),
            *TensorReduce.semaphores(),
            dma((steps,)), dma((steps,)), dma((len(rights),)), dma((2,)), dma((1 + 2 * len(digit_sizes(n)),)),
        ],
        compiler_params=pltpu.CompilerParams(vmem_limit_bytes=VMEM_BYTES, has_side_effects=True),
        cost_estimate=pl.CostEstimate(
            flops=2 * tokens * features * sum(columns), bytes_accessed=4 * features * sum(columns), transcendentals=0
        ),
        name="finish",
    )(
        part, part_out, middle, d_middle, stream, gain, gain_grad_two,
        *[column_blocks(v, n) for v in lefts], *rights, *[g for item in given for g in item],
    )
    return results[0], results[1], results[2 : 2 + len(rights)], results[-1]


class TensorGather:
    def __init__(self, line, own_v, out, send_sem, recv_sem):
        self.line, self.own_v, self.out, self.rows = line, own_v, out, own_v.shape[0]
        self.over = remote(own_v, self.block(line.index), send_sem.at[0], recv_sem.at[0], "tensor", line.peer)
        self.aside = remote(own_v, self.block(line.index), send_sem.at[1], recv_sem.at[1], "tensor", line.mate)
        self.onward = remote(self.block(line.peer), self.block(line.peer), send_sem.at[2], recv_sem.at[2], "tensor", line.mate)

    def block(self, index):
        return self.out.at[pl.ds(pl.multiple_of(index * self.rows, self.rows), self.rows)]

    def start(self):
        self.over.start()
        self.aside.start()

    def forward(self):
        self.over.wait_recv()
        self.onward.start()

    def drain(self):
        for copy in (self.over, self.aside, self.onward):
            copy.wait_send()

    @staticmethod
    def semaphores():
        return [pltpu.SemaphoreType.DMA((3,)), pltpu.SemaphoreType.DMA((3,))]


def forward_kernel(*refs):
    take = Reader(refs)
    cot_own, w_gate, w_branch, w_out = take(4)
    stream, gain, gain_two, masks, vecs, w_cat = take(6)
    normed, cot, gated_o, branch_o, conv_o, states_o, product_o, middle_o, normed_two, from_mate, from_peer = take(11)
    wg_v, wb_v, wo_v, own_v, cot_v, block_v, gated_v, branch_v, conv_v, states_v, product_v = take(11)
    pre_s, a_s, b_s, part_v, rs_own, rs_got, rs_send_v, middle_v, two_v = take(9)
    ag_sems, cot_sems, two_sems = take(2), take(2), take(2)
    rs_send, rs_recv, rs_sem, sem = take(4)
    rows, features = stream.shape
    line = TensorLine()
    gather = TensorGather(line, own_v, normed, *ag_sems)
    cots = TensorGather(line, cot_v, cot, *cot_sems)
    twos = TensorGather(line, two_v, normed_two, *two_sems)
    reduce = TensorReduce(line, part_v, from_mate, from_peer, rs_own, rs_got, rs_send_v, rs_send, rs_recv, rs_sem)
    loads = [copy_in(w_gate, wg_v, sem.at[0]), copy_in(w_branch, wb_v, sem.at[1]), copy_in(w_out, wo_v, sem.at[2])]
    cot_load = copy_in(cot_own, cot_v, sem.at[3])

    def chunks(body):
        @pl.loop(0, rows // 16)
        def _(r):
            body(pl.ds(pl.multiple_of(r * 16, 16), 16))

    def norm(values, gains):
        inverse = lax.rsqrt(jnp.mean(values * values, axis=-1, keepdims=True) + epsilon)
        return (values * inverse * gains).astype(BF16)

    def first_norm(at):
        own_v[at, :] = norm(stream[at, :].astype(F32), gain[...])

    chunks(first_norm)
    gather.start()
    keep = [copy_in(own_v, gather.block(line.index), sem.at[4])]
    cot_load.wait()
    cots.start()
    keep.append(copy_in(cot_v, cots.block(line.index), sem.at[5]))

    def project(source, index):
        at = pl.ds(pl.multiple_of(index * rows, rows), rows)
        branch_v[at, :] = jnp.dot(source, wb_v[...], preferred_element_type=F32)
        gated_v[at, :] = jnp.dot(source, wg_v[...], preferred_element_type=F32)

    loads[0].wait()
    loads[1].wait()
    project(own_v[...], line.index)
    gather.aside.wait_recv()
    copy_in(gather.block(line.mate), block_v.at[0], sem.at[6]).wait()
    project(block_v[0], line.mate)
    gather.forward()
    copy_in(gather.block(line.peer), block_v.at[1], sem.at[6]).wait()
    project(block_v[1], line.peer)
    gather.onward.wait_recv()
    copy_in(gather.block(line.cross), block_v.at[0], sem.at[6]).wait()
    project(block_v[0], line.cross)
    outs = [copy_in(branch_v, branch_o, sem.at[7]), copy_in(gated_v, gated_o, sem.at[8])]
    mixer_forward_kernel(branch_v, gated_v, masks, vecs, w_cat, conv_v, states_v, product_v, pre_s, a_s, b_s)
    outs += [copy_in(conv_v, conv_o, sem.at[9]), copy_in(states_v, states_o, sem.at[10]), copy_in(product_v, product_o, sem.at[11])]
    loads[2].wait()

    def out_block(index):
        at = pl.ds(pl.multiple_of(index * rows, rows), rows)
        part_v[at, :] = jnp.dot(product_v[at, :], wo_v[...], preferred_element_type=F32).astype(BF16)

    out_block(line.cross)
    reduce.mates[0].start()
    out_block(line.peer)
    reduce.middle()
    out_block(line.mate)
    reduce.mates[1].start()
    out_block(line.index)
    cots.forward()

    def second_norm(at, total):
        values = stream[at, :].astype(F32) + total
        middle_v[at, :] = values
        two_v[at, :] = norm(values, gain_two[...])

    reduce.end(second_norm)
    twos.start()
    keep += [copy_in(two_v, twos.block(line.index), sem.at[12]), copy_in(middle_v, middle_o, sem.at[13])]
    cots.aside.wait_recv()
    cots.onward.wait_recv()
    twos.forward()
    twos.aside.wait_recv()
    twos.onward.wait_recv()
    for copy in keep + outs:
        copy.wait()
    for gathered in (gather, cots, twos):
        gathered.drain()
    reduce.drain()


def forward(cot_own, w_gate, w_branch, w_out, stream, gain, gain_two, masks, vecs, w_cat):
    rows, features = stream.shape
    tokens, channels = 4 * rows, w_gate.shape[1]
    lanes = channels // LANES
    whole = jax.ShapeDtypeStruct((tokens, features), BF16)
    wide = jax.ShapeDtypeStruct((tokens, channels), F32)
    narrow = jax.ShapeDtypeStruct((tokens, channels), BF16)
    results = [whole, whole, wide, wide, narrow, wide, narrow, jax.ShapeDtypeStruct((rows, features), F32), whole]
    results += TensorReduce.results(tokens, features)
    block = pltpu.VMEM((rows, features), BF16)
    return pl.pallas_call(
        forward_kernel,
        out_shape=results,
        in_specs=[HBM] * 4 + [IN_VMEM] * 6,
        out_specs=[HBM] * len(results),
        scratch_shapes=[
            pltpu.VMEM(w_gate.shape, BF16), pltpu.VMEM(w_branch.shape, BF16), pltpu.VMEM(w_out.shape, BF16),
            block, block, pltpu.VMEM((2, rows, features), BF16),
            pltpu.VMEM((tokens, channels), F32), pltpu.VMEM((tokens, channels), F32),
            pltpu.VMEM((tokens, channels), BF16), pltpu.VMEM((tokens, channels), F32), pltpu.VMEM((tokens, channels), BF16),
            pltpu.VMEM((tokens, 2 * channels), F32),
            pltpu.VMEM((lanes, tokens, LANES), F32), pltpu.VMEM((lanes, tokens, LANES), F32),
            pltpu.VMEM((tokens, features), BF16), *TensorReduce.buffers(tokens, features),
            pltpu.VMEM((rows, features), F32), block,
            *TensorGather.semaphores(), *TensorGather.semaphores(), *TensorGather.semaphores(),
            *TensorReduce.semaphores(), pltpu.SemaphoreType.DMA((14,)),
        ],
        compiler_params=pltpu.CompilerParams(vmem_limit_bytes=VMEM_BYTES, has_side_effects=True),
        cost_estimate=pl.CostEstimate(flops=9 * 10**9, bytes_accessed=40 * 10**6, transcendentals=6 * tokens * channels),
        name="forward",
    )(cot_own, w_gate, w_branch, w_out, stream, gain, gain_two, masks, vecs, w_cat)

DP_PLAN = [True, False, False, False, False, False]
DP_ORDER = [2, -1, 1, 1, -1, 4, 5, 3, 1, 2, 2, -1, -1, 4, -1, 4, 0, 2, 5, -1, 1, -1, 5, 4, 3, -1, 5, 2, -1, 3, 0, 4, 3, -1, 5, 3]


def dot(left, right, dims, out=F32):
    return lax.dot_general(left, right, (dims, ((), ())), preferred_element_type=F32).astype(out)


def spread_heads(*weights):
    heads, width = weights[0].shape[:2]
    total = len(weights) * heads * width
    rows = []
    for h in range(heads):
        row = 0
        for q, weight in enumerate(weights):
            before = (q * heads + h) * width
            row = row + jnp.pad(weight[h], ((0, 0), (before, total - before - width)))
        rows.append(row)
    return jnp.concatenate(rows)


def head_blocks(dense, heads, width):
    return jnp.stack([dense[h * width : (h + 1) * width, h * width : (h + 1) * width] for h in range(heads)])


def on_device(
    stream_in, segments, first_gain, gelu_gate_weight, recurrent_branch_weight, conv_kernel, conv_bias, recur_weight, recur_bias,
    inlet_weight, inlet_bias, decay_param, recurrent_output_weight, second_gain, gate_projection_weight, up_projection_weight,
    down_projection_weight, cotangent,
):
    seq_len = segments.shape[1]
    heads, head_width = recur_weight.shape[:2]
    ids = jnp.pad(segments[0], (3, 8), constant_values=-1)
    same = [(ids[3 - k : 3 - k + seq_len] == segments[0]).astype(F32) for k in range(1, 4)]
    masks = jnp.pad(jnp.stack(same, axis=1), ((0, 8), (0, 5)))
    softplus = jax.nn.softplus(-decay_param)
    vecs = jnp.concatenate([conv_kernel, jnp.stack([conv_bias, recur_bias, inlet_bias, softplus])])
    w_cat = spread_heads(recur_weight, inlet_weight)

    normed, cot, gated_pre, branch_pre, conv_out, states, product, middle, normed_two, _, _ = forward(
        cotangent[0], gelu_gate_weight, recurrent_branch_weight, recurrent_output_weight, stream_in[0], first_gain[None],
        second_gain[None], masks, vecs, w_cat,
    )
    gate_pre = dot(normed_two, gate_projection_weight, ((1,), (0,)))
    up_pre = dot(normed_two, up_projection_weight, ((1,), (0,)))
    gate_act, gate_slope = gelu_parts(gate_pre)
    hidden = (gate_act * up_pre).astype(BF16)
    d_hidden = dot(cot, down_projection_weight, ((1,), (1,)))
    d_gate = (d_hidden * up_pre * gate_slope).astype(BF16)
    d_up = (d_hidden * gate_act).astype(BF16)
    part_two = (dot(d_gate, gate_projection_weight, ((1,), (1,))) + dot(d_up, up_projection_weight, ((1,), (1,)))).astype(BF16)
    part_out = dot(hidden, down_projection_weight, ((1,), (0,)), BF16)
    d_middle, d_attended, d_gated, d_ri, d_branch, _, _, down_got, gate_got, sums, gain_two = chain(
        part_two, middle, cotangent[0], recurrent_output_weight, gated_pre, branch_pre, states, conv_out,
        second_gain[None], masks, vecs, w_cat, cot, normed_two, hidden, d_gate,
    )
    part_one = (dot(d_gated, gelu_gate_weight, ((1,), (1,))) + dot(d_branch, recurrent_branch_weight, ((1,), (1,)))).astype(BF16)
    stream_grad, stream_out, gradients, gains = finish(
        part_one, part_out, middle, d_middle, stream_in[0], first_gain[None], gain_two,
        [cot, normed_two, d_attended, normed], [0, 1, 1, 2, 3, 3], [hidden, d_gate, d_up, product, d_gated, d_branch],
        [[down_got], [gate_got], [], [], [], []], DP_PLAN, DP_ORDER,
    )
    down_gradient, gate_gradient, up_gradient, output_gradient, gated_gradient, branch_gradient = gradients

    width = heads * head_width
    dense = dot(conv_out, d_ri, ((0,), (0,)))
    grad_recur = head_blocks(dense[:, :width], heads, head_width)
    grad_inlet = head_blocks(dense[:, width:], heads, head_width)
    sums = jnp.sum(sums, axis=1)
    small = jnp.concatenate([sums.reshape(-1), grad_recur.reshape(-1), grad_inlet.reshape(-1)])
    small = lax.psum(small, "dp")
    sums = small[: 8 * width].reshape(8, width)
    grad_recur, grad_inlet = small[8 * width :].reshape(2, heads, head_width, head_width)
    grad_decay = decay_scale * jax.nn.sigmoid(-decay_param) * sums[7]
    return (
        stream_out[None], stream_grad[None], gains[0], gated_gradient, branch_gradient, sums[:4], sums[4], grad_recur, sums[5],
        grad_inlet, sums[6], grad_decay, output_gradient.T, gains[1], gate_gradient, up_gradient, down_gradient.T,
    )


def solution(mesh):
    in_specs = (
        P("dp", "tensor", None),
        P("dp", None),
        P(),
        P(None, "tensor"),
        P(None, "tensor"),
        P(None, "tensor"),
        P("tensor"),
        P("tensor", None, None),
        P("tensor"),
        P("tensor", None, None),
        P("tensor"),
        P("tensor"),
        P("tensor", None),
        P(),
        P(None, "tensor"),
        P(None, "tensor"),
        P("tensor", None),
        P("dp", "tensor", None),
    )
    out_specs = (
        P("dp", "tensor", None),
        P("dp", "tensor", None),
        P(),
        P("dp", "tensor"),
        P("dp", "tensor"),
        P(None, "tensor"),
        P("tensor"),
        P("tensor", None, None),
        P("tensor"),
        P("tensor", None, None),
        P("tensor"),
        P("tensor"),
        P("tensor", "dp"),
        P(),
        P("dp", "tensor"),
        P("dp", "tensor"),
        P("tensor", "dp"),
    )
    return jax.shard_map(
        on_device, mesh=mesh, in_specs=in_specs, out_specs=out_specs, check_vma=False
    )
```

time: 880 us -> 647 us (0.74)
  waiting for transfers between devices: 195 us -> 0.02 us
  Pallas kernels: 444 us -> 505 us
  matrix products: 127 us -> 80.8 us
  blocking collectives: 41.6 us -> 0 us
  other arithmetic: 27.4 us -> 7.51 us
    all_gather x4 -> x0, waiting for transfers between devices: 105 us -> none  [on_device(): gather = lambda v: lax.all_gather(v, 'tensor', axis=0, tiled=True)]
    reduce_scatter x4 -> x0, waiting for transfers between devices: 89 us -> none  [on_device(): lax.psum_scatter(v, 'tensor', scatter_dimension=0, tiled=True).astype(F32)]
    pallas_call x3, Pallas kernels: 444 us -> 505 us  [the longest x1 230 us: finish(): pl.pallas_call(functools.partial(finish_kernel, n, width, plan, task_orde...]
    dot_general x13 -> x9, matrix products: 127 us -> 80.8 us  [dot(): lax.dot_general(left, right, (dims, ((), ())), preferred_element_type=F32)]
    psum x1 -> x0, blocking collectives: 41.6 us -> none  [on_device(): lax.psum(jnp.concatenate([grad_first, grad_second]), ('dp', 'tensor'))]
  transfers between devices with their start and end apart: 9 -> 1, of which waited for: 6 -> 0; matrix products, arithmetic and copies ran while one was open for 8% -> 4% of each run, Pallas kernels for 44% -> 36%
where the time goes in v2:
time: 647 us; the launch traced here: 635 us
  Pallas kernels  505 us (78%)
  matrix products  80.8 us (12%)
  local copies, waits for them, and re-layouts  26.6 us (4%)
  between operations  14.8 us (2%)
  other arithmetic  7.51 us (1%)
    pallas_call x1, Pallas kernels, finish(): pl.pallas_call(functools.partial(finish_kernel, n, width, plan, task_orde...  230 us
    pallas_call x1, Pallas kernels, chain(): pl.pallas_call(functools.partial(chain_kernel, n, width), out_shape=[jax....  152 us
    pallas_call x1, Pallas kernels, forward(): pl.pallas_call(forward_kernel, out_shape=results, in_specs=[HBM] * 4 + [I...  124 us
    dot_general x9, matrix products, dot(): lax.dot_general(left, right, (dims, ((), ())), preferred_element_type=F32)  80.8 us
    unnamed x44, local copies, waits for them, and re-layouts  13.8 us
  transfers between devices with their start and end apart: 1, of which 0 were waited for; matrix products, arithmetic and copies ran while one was open for 4% of the time, Pallas kernels for 36%

profile of v2, /device:TPU:0, one launch (start us, length us, event | category | flops | bytes accessed | tf_op | source)
XLA Modules:
  0.0 634.7 jit_solution(10979299425002815709)
XLA Ops:
  9.3 0.9 fusion.1
  11.3 1.0 slice_bitcast_fusion.15
  12.3 1.0 slice_bitcast_fusion.14
  13.4 0.8 pad_convert_fusion.refs_7_.refs_9_
  14.6 1.3 pad_maximum_fusion.refs_9_.refs_11_
  16.5 123.6 %forward.1 = (bf16[1024,2048]{1,0:T(8,128)(2,1)}, bf16[1024,2048]{1,0:T(8,128)(2,1)}, f32[1024,640]{1,0:T(8,128)}, f32[1024,640]{1,0:T(8,128)}, bf16[1024,640]{1...) custom-call(bf16[256,2048]{1,0:T(8,128)(2,1)} %bitcast.72, ...), custom_call_target="tpu_custom_call" | custom-call | flops 8999999488 | bytes 40000000 | tf_op jit(solution)/shard_map/forward/pallas_call | solution.py:1078
  140.1 12.1 %fusion.6 = f32[1024,1536]{1,0:T(8,128)} fusion(bf16[1024,2048]{1,0:T(8,128)(2,1)} %get-tuple-element.44.refs_12_.refs_7_, bf16[1536,2048]{1,0:T(8,128)(2,1)} %param.34), kind=kOutput, calls=%fused_computation.45 | convolution fusion | flops 6442450944 | bytes 16777216 | tf_op jit(solution)/shard_map/dot_general | solution.py:1105
  152.3 8.6 %fusion.7 = f32[1024,1536]{1,0:T(8,128)} fusion(bf16[1024,2048]{1,0:T(8,128)(2,1)S(1)} %copy-done.12, bf16[2048,1536]{1,0:T(8,128)(2,1)S(1)} %bitcast.69), kind=kOutput, calls=%fused_computation.46 | convolution fusion | flops 6442450944 | bytes 16777216 | tf_op jit(solution)/shard_map/dot_general | solution.py:1105
  160.9 15.3 %multiply_convert_fusion = (bf16[1024,1536]{1,0:T(8,128)(2,1)}, bf16[1024,1536]{1,0:T(8,128)(2,1)}, bf16[1024,1536]{1,0:T(8,128)(2,1)}) fusion(f32[1024,1536]{1,0:T(8,128)} %fusion.7, f32[1024,1536]{1,0:T(8,128)} %fusion.6, bf16[1024,2048]{1,0:T(8,128)(2,1)S(1)} %copy-done.12, bf16[2048,1536]{1,0:T(8,128)(2,1)S(1)} %bitcast.71), kind=kOutput, calls=%fused_computation.2 | convolution fusion | flops 6480199680 | bytes 32505856 | tf_op jit(solution)/shard_map/dot_general | solution.py:1105
  176.2 10.5 %fusion.8 = f32[1024,2048]{1,0:T(8,128)} fusion(bf16[1024,1536]{1,0:T(8,128)(2,1)} %get-tuple-element.123.refs_15_.refs_12_, bf16[2048,1536]{1,0:T(8,128)(2,1)S(1)} %bitcast.69), kind=kOutput, calls=%fused_computation.47 | convolution fusion | flops 6442450944 | bytes 17825792 | tf_op jit(solution)/shard_map/dot_general | solution.py:1105
  186.7 10.9 %add_convert_fusion.1.refs_0_ = bf16[1024,2048]{1,0:T(8,128)(2,1)} fusion(f32[1024,2048]{1,0:T(8,128)} %fusion.8, bf16[1024,1536]{1,0:T(8,128)(2,1)S(1)} %copy-done.13, bf16[2048,1536]{1,0:T(8,128)(2,1)S(1)} %bitcast.71), kind=kOutput, calls=%fused_computation.1 | convolution fusion | flops 6446645248 | bytes 22020096 | tf_op jit(solution)/shard_map/dot_general | solution.py:1105
  197.6 151.8 %chain.1 = (f32[256,2048]{1,0:T(8,128)}, bf16[1024,2048]{1,0:T(8,128)(2,1)}, bf16[1024,640]{1,0:T(8,128)(2,1)}, bf16[1024,1280]{1,0:T(8,128)(2,1)}, bf16[1024,64...) custom-call(bf16[1024,2048]{1,0:T(8,128)(2,1)} %add_convert_fusion.1, ...), custom_call_target="tpu_custom_call" | custom-call | flops 12000000000 | bytes 60000000 | tf_op jit(solution)/shard_map/chain/pallas_call | solution.py:735
  349.4 1.0 reduce_sum.9
  350.4 3.7 fusion.10
  355.5 1.0 pad_maximum_fusion.1
  356.5 11.2 %convolution_convert_fusion.refs_1_ = bf16[1024,2048]{1,0:T(8,128)(2,1)} fusion(bf16[1024,1536]{1,0:T(8,128)(2,1)} %get-tuple-element.122.refs_14_.refs_11_, bf16[1536,2048]{1,0:T(8,128)(2,1)} %param.34), kind=kOutput, calls=%fused_computation.8 | convolution fusion | flops 6444548096 | bytes 13631488 | tf_op jit(solution)/shard_map/dot_general | solution.py:1105
  367.8 3.4 fusion.9
  371.2 5.0 add_convert_fusion.refs_0_
  376.3 229.6 %finish.1 = (f32[256,2048]{1,0:T(8,128)}, f32[256,2048]{1,0:T(8,128)}, f32[256,1536]{1,0:T(8,128)}, f32[256,1536]{1,0:T(8,128)}, f32[256,1536]{1,0:T(8,128)}, /*...) custom-call(bf16[1024,2048]{1,0:T(8,128)(2,1)} %add_convert_fusion.r, ...), custom_call_target="tpu_custom_call" | custom-call | flops 27380416512 | bytes 53477376 | tf_op jit(solution)/shard_map/finish/pallas_call | solution.py:914
  605.9 2.2 copy.43
  608.0 3.0 copy.44
  611.1 1.6 fusion.5
  614.0 1.2 fusion.4
  615.2 1.1 unstack.15
  616.3 1.1 unstack.13
  617.5 1.4 slice_multiply_fusion
  618.9 3.2 copy.52
  622.2 1.3 copy.53
  623.5 0.8 copy.54
  624.3 0.8 copy.55
  625.2 1.1 copy.56
  626.3 1.1 copy.57
  (62 shorter events, 6.9 us)
Async XLA Ops:
  7.2 8.6 %copy-start.7 = (f32[4,640]{1,0:T(4,128)S(1)}, f32[4,640]{1,0:T(4,128)}, u32[]{:S(2)}) copy-start(f32[4,640]{1,0:T(4,128)} %param.23) | copy-start | bytes 30724
  7.2 605.5 %all-reduce.12.cloned.1.call-start = ((), (), s32[]{:S(2)}) async-start(), calls=%async_computation | async-start | bytes 1679360 | tf_op jit(solution)/shard_map/psum | solution.py:1170
  16.5 135.8 %slice-start = ((s8[6291456]{0:T(1024)(128)(4,1)}), s8[2097152]{0:T(1024)(128)(4,1)S(1)}, s32[]{:S(2)}) async-start(s8[6291456]{0:T(1024)(128)(4,1)} %bitcast.68), calls=%async_computation.1 | async-start | bytes 4194304
  140.1 12.2 %slice-start.1 = ((s8[6291456]{0:T(1024)(128)(4,1)}), s8[4194304]{0:T(1024)(128)(4,1)S(1)}, s32[]{:S(2)}) async-start(s8[6291456]{0:T(1024)(128)(4,1)} %bitcast.68), calls=%async_computation.2 | async-start | bytes 8388608
  140.1 12.2 %copy-start.12 = (bf16[1024,2048]{1,0:T(8,128)(2,1)S(1)}, bf16[1024,2048]{1,0:T(8,128)(2,1)}, u32[]{:S(2)}) copy-start(bf16[1024,2048]{1,0:T(8,128)(2,1)} %get-tuple-element.45.refs_13_.refs_8_) | copy-start | bytes 12582916
  140.1 20.8 %slice-start.2 = ((s8[6291456]{0:T(1024)(128)(4,1)}), s8[4194304]{0:T(1024)(128)(4,1)S(1)}, s32[]{:S(2)}) async-start(s8[6291456]{0:T(1024)(128)(4,1)} %bitcast.70), calls=%async_computation.3 | async-start | bytes 8388608
  152.3 8.6 %slice-start.3 = ((s8[6291456]{0:T(1024)(128)(4,1)}), s8[2097152]{0:T(1024)(128)(4,1)S(1)}, s32[]{:S(2)}) async-start(s8[6291456]{0:T(1024)(128)(4,1)} %bitcast.70), calls=%async_computation.4 | async-start | bytes 4194304
  176.2 10.5 %copy-start.13 = (bf16[1024,1536]{1,0:T(8,128)(2,1)S(1)}, bf16[1024,1536]{1,0:T(8,128)(2,1)}, u32[]{:S(2)}) copy-start(bf16[1024,1536]{1,0:T(8,128)(2,1)} %get-tuple-element.124.refs_13_) | copy-start | bytes 9437188
  197.6 152.8 %copy-start.3 = (bf16[1024,640]{1,0:T(8,128)(2,1)S(1)}, bf16[1024,640]{1,0:T(8,128)(2,1)}, u32[]{:S(2)}) copy-start(bf16[1024,640]{1,0:T(8,128)(2,1)} %get-tuple-element.50.refs_7_) | copy-start | bytes 3932164
  356.5 11.3 %copy-start.8 = (bf16[2048,640]{1,0:T(8,128)(2,1)S(1)}, bf16[2048,640]{1,0:T(8,128)(2,1)}, u32[]{:S(2)}) copy-start(bf16[2048,640]{1,0:T(8,128)(2,1)} %refs_1_.1) | copy-start | bytes 7864324
  356.5 11.2 %copy-start.11 = (bf16[1024,640]{1,0:T(8,128)(2,1)S(1)}, bf16[1024,640]{1,0:T(8,128)(2,1)}, u32[]{:S(2)}) copy-start(bf16[1024,640]{1,0:T(8,128)(2,1)} %get-tuple-element.51.refs_15_) | copy-start | bytes 3932164
  367.8 3.5 copy-start.9
  367.8 3.5 copy-start.10
  605.9 11.6 %copy-start.6 = (f32[640]{0:T(1024)S(1)}, f32[640]{0:T(1024)}, u32[]{:S(2)}) copy-start(f32[640]{0:T(1024)} %param.29) | copy-start | bytes 7684
  611.1 11.1 %copy-start = (f32[256,2048]{1,0:T(8,128)S(1)}, f32[256,2048]{1,0:T(8,128)}, u32[]{:S(2)}) copy-start(f32[256,2048]{1,0:T(8,128)} %get-tuple-element.61) | copy-start | bytes 6291460
  618.9 4.6 copy-start.5
  618.9 5.4 copy-start.4
  622.2 3.0 copy-start.2
  622.2 4.1 copy-start.1
Sparse Core Ops, SparseCore 0:
  356.6 79.0 all-reduce.11
